TPU v7x, 256 devices: a whole 4x4x8 slice. The times are simulated.
256 devices in a mesh: mem: 64 (over x, z, core), blk: 4 (over y).
Axes of the slice: x: 4, y: 4, z: 8, core: 2. Of those that a mesh axis runs over, the one named last changes fastest.
Arguments:
- ensemble: bfloat16 [128, 1048576], P('mem', 'blk'), may hold values from -6 to 6
- obs_cell: int32 [4, 512, 256], P('blk', 'mem'), may hold values from 0 to 511
- obs_count: int32 [4, 512], P('blk', 'mem'), may hold values from 1 to 256, 81920 in all within a row
- obs_value: float32 [4, 512, 256], P('blk', 'mem'), may hold values from -6 to 6
- obs_rinv: float32 [4, 512, 256], P('blk', 'mem'), may hold values from 0.05 to 0.5
Outputs:
- increments: bfloat16 [128, 1048576], P('mem', 'blk')
Inputs may be any that keep to these rules, and one draw needn't show every extreme that they name: `obs_cell`: slots at or past the block's count are unused. `obs_count`: the counts of one band sum to 81920, and some block holds exactly 256.
All inputs are finite; a program needn't handle non-finite values. Where the computation divides by a largest or mean magnitude, that divisor is 1e-20 or more.
Results may differ from a plain program's by a relative error of at most 0.0051.
Values may be sent and summed in bfloat16 or wider, within the bound.
No kernel may reach another device: no remote copies, remote signals or barrier semaphores. Data moves between devices by JAX's collectives and lax.ppermute only.
A program may use at most 64 MiB of HBM per device.

v0:
```python
import jax
import jax.numpy as jnp
from jax import lax
from jax.sharding import PartitionSpec as P

NS_ITERS = 4


localize = 0.5
inflation = 1.1


def with_halo(block, sides, width):
    for axis, dim in sides:
        count = lax.axis_size(axis)
        forward = [(i, i + 1) for i in range(count - 1)]
        forward.append((count - 1, 0))
        backward = [(target, source) for source, target in forward]
        low = lax.ppermute(
            lax.slice_in_dim(block, block.shape[dim] - width, None, axis=dim), axis, forward
        )
        high = lax.ppermute(lax.slice_in_dim(block, 0, width, axis=dim), axis, backward)
        block = jnp.concatenate([low, block, high], axis=dim)
    return block


def center_blocks(members):
    values = jnp.transpose(members.astype(jnp.float32), (1, 0, 2))
    average = jnp.mean(values, axis=1)
    return (values - average[:, None, :], average)


def observe(deviation, average, cell_ids, live_counts, obs_values, inv_var):
    cell_width = deviation.shape[2]
    positions = lax.broadcasted_iota(jnp.int32, cell_ids.shape + (cell_width,), 2)
    selector = (positions == cell_ids[:, :, None]).astype(jnp.float32)
    sampled = jnp.einsum("bkc,boc->bko", deviation, selector, precision=lax.Precision.HIGHEST)
    obs_mean = jnp.einsum("bc,boc->bo", average, selector, precision=lax.Precision.HIGHEST)
    slots = lax.broadcasted_iota(jnp.int32, cell_ids.shape, 1)
    live = (slots < live_counts[:, None]).astype(jnp.float32)
    weight_root = live * jnp.sqrt(inv_var)
    upper = sampled * weight_root[:, None, :]
    lower = (weight_root * (obs_values - obs_mean))[:, None, :]
    return jnp.concatenate([upper, lower], axis=1).astype(jnp.bfloat16)


def gram_of(obs_rows):
    return jnp.einsum("bko,bjo->bkj", obs_rows, obs_rows, preferred_element_type=jnp.float32)


def batch_mm(left, right):
    return jnp.einsum("bij,bjk->bik", left, right, precision=lax.Precision.HIGHEST)


def transform_apply(localized, deviation):
    ensemble_size = deviation.shape[1]
    identity = jnp.eye(ensemble_size, dtype=jnp.float32)
    system = (ensemble_size - 1) / inflation * identity + localized[
        :, :ensemble_size, :ensemble_size
    ]
    forcing = localized[:, :ensemble_size, ensemble_size]
    bound_norm = jnp.max(jnp.sum(jnp.abs(system), axis=2), axis=1)
    approx_y = system / bound_norm[:, None, None]
    approx_z = jnp.broadcast_to(identity, system.shape)
    for iteration in range(NS_ITERS):
        update = 1.5 * identity - 0.5 * batch_mm(approx_z, approx_y)
        approx_y = batch_mm(approx_y, update)
        approx_z = batch_mm(update, approx_z)
    root_inv = approx_z / jnp.sqrt(bound_norm)[:, None, None]
    inner = jnp.einsum("bij,bj->bi", root_inv, forcing, precision=lax.Precision.HIGHEST)
    mean_weights = jnp.einsum("bij,bj->bi", root_inv, inner, precision=lax.Precision.HIGHEST)
    mixing = (
        jnp.sqrt(jnp.float32(ensemble_size - 1)) * root_inv + mean_weights[:, :, None] - identity
    )
    increment = jnp.einsum("bjc,bjk->kbc", deviation, mixing, precision=lax.Precision.HIGHEST)
    return increment.astype(jnp.bfloat16)


def on_device(ensemble, obs_cell, obs_count, obs_value, obs_rinv):
    groups = lax.axis_size("mem")
    local_members = ensemble.shape[0]
    blocks = obs_cell.shape[1]
    cell_width = ensemble.shape[1] // (groups * blocks)
    pieces = ensemble.reshape(local_members, groups, blocks, cell_width)
    arrived = lax.all_to_all(pieces, "mem", split_axis=1, concat_axis=0, tiled=True)
    deviation, average = center_blocks(arrived[:, 0])
    obs_rows = observe(deviation, average, obs_cell[0], obs_count[0], obs_value[0], obs_rinv[0])
    padded_rows = with_halo(obs_rows, (("mem", 0),), 1)
    padded = gram_of(padded_rows)
    localized = padded[1:-1] + localize * (padded[:-2] + padded[2:])
    increment = transform_apply(localized, deviation)
    ensemble_size = increment.shape[0]
    outgoing = increment.reshape(ensemble_size, 1, blocks * cell_width)
    returned = lax.all_to_all(outgoing, "mem", split_axis=0, concat_axis=1, tiled=True)
    return returned.reshape(local_members, groups * blocks * cell_width)


def solution(mesh):
    placed = (
        P("mem", "blk"),
        P("blk", "mem", None),
        P("blk", "mem"),
        P("blk", "mem", None),
        P("blk", "mem", None),
    )
    return jax.shard_map(
        on_device, mesh=mesh, in_specs=placed, out_specs=P("mem", "blk"), check_vma=False
    )
```

profile of v0, /device:TPU:1, one launch (start us, length us, event | category | flops | bytes accessed | tf_op | source)
XLA Modules:
  0.0 120.8 jit_solution(8806830883957648730)
XLA Ops:
  0.0 1.4 %copy.84 = bf16[1,2,512,512]{3,2,1,0:T(8,128)(2,1)S(1)} copy(bf16[1,2,512,512]{3,1,2,0:T(2,128)(2,1)} %bitcast.89) | data formatting | bytes 2097152
  1.4 1.1 copy.42
  2.5 13.0 %all-to-all-start = ((bf16[2,64,8,512]{3,2,0,1:T(8,128)(2,1)}), bf16[2,64,8,512]{3,2,0,1:T(8,128)(2,1)S(1)}, u32[]{:S(2)}, u32[]{:S(2)}) async-start(bf16[2,64,8,512]{3,2,0,1:T(8,128)(2,1)} %copy.42), calls=%async_computation | async-start | bytes 2097152 | tf_op jit(solution)/shard_map/all_to_all | solution.py:85
  15.7 28.3 %all-to-all-done = bf16[2,64,8,512]{3,2,0,1:T(8,128)(2,1)S(1)} async-done(((bf16[2,64,8,512]{3,2,0,1:T(8,128)(2,1)}), bf16[2,64,8,512]{3,2,0,1:T(8,128)(2,1)S(1)}, u32[]{:S(2)}, u32[]{:S(2)}) %all-to-all-start) | async-done | bytes 1048608 | tf_op jit(solution)/shard_map/all_to_all | solution.py:85
  44.4 1.1 bitcast_reduce_fusion
  45.6 2.2 %fusion = f32[8,1,256]{2,1,0:T(1,128)S(1)} fusion(s32[8,256]{1,0:T(8,128)S(1)} %bitcast.92, f32[8,512,1]{1,0,2:T(8,128)S(1)} %get-tuple-element.9), kind=kOutput, calls=%fused_computation.1 | convolution fusion | flops 13631488 | bytes 32768 | tf_op jit(solution)/shard_map/bc,boc->bo/dot_general | solution.py:38
  47.9 3.5 %fusion.10 = bf16[8,128,256]{2,1,0:T(8,128)(2,1)S(1)} fusion(s32[8,256]{1,0:T(8,128)S(1)} %bitcast.93, f32[128,8,512]{2,1,0:T(8,128)S(1)} %bitcast.85, f32[8,512]{1,0:T(8,128)S(1)} %get-tuple-element.10, f32[8,256]{1,0:T(8,128)S(1)} %get-tuple-element.6), kind=kOutput, calls=%fused_computation.13 | convolution fusion | flops 1612709888 | bytes 2654208 | tf_op jit(solution)/shard_map/bkc,boc->bko/dot_general | solution.py:37
  51.4 1.0 collective-permute-start
  52.4 1.4 %collective-permute-done = bf16[1,129,256]{2,1,0:T(8,128)(2,1)S(1)} collective-permute-done((bf16[1,129,256]{2,1,0:T(8,128)(2,1)S(1)}, bf16[1,129,256]{2,1,0:T(8,128)(2,1)S(1)}, u32[]{:S(2)}, u32[]{:S(2)}) %collective-permute-start) | collective-permute-done | bytes 66080 | tf_op jit(solution)/shard_map/ppermute | solution.py:19
  53.8 2.4 %collective-permute-done.1 = bf16[1,129,256]{2,1,0:T(8,128)(2,1)S(1)} collective-permute-done((bf16[1,129,256]{2,1,0:T(8,128)(2,1)S(1)}, bf16[1,129,256]{2,1,0:T(8,128)(2,1)S(1)}, u32[]{:S(2)}, u32[]{:S(2)}) %collective-permute-start.1) | collective-permute-done | bytes 66080 | tf_op jit(solution)/shard_map/ppermute | solution.py:22
  56.8 1.3 %fusion.14 = f32[8,128,128]{2,1,0:T(8,128)S(1)} fusion(f32[128,128]{1,0:T(8,128)S(1)} %copy.41, f32[128,128]{1,0:T(8,128)S(1)} %copy.40, f32[8,129,129]{1,2,0:T(8,128)S(1)} %fusion.16, f32[8]{0:T(128)S(1)} %reduce_max.9, f32[128,128]{0,1:T(8,128)S(1)} %fusion.37), kind=kOutput, calls=%fused_computation.22 | convolution fusion | flops 201850880 | bytes 1245696 | tf_op jit(solution)/shard_map/bij,bjk->bik/dot_general | solution.py:52
  58.1 1.1 fusion.48
  59.8 0.6 fusion.13
  61.7 0.6 fusion.12
  65.0 0.9 convolution_bitcast_fusion
  65.9 0.9 fusion.55
  66.9 3.4 %fusion.8 = bf16[128,8,512]{2,0,1:T(8,128)(2,1)S(1)} fusion(f32[128,8,512]{2,1,0:T(8,128)S(1)} %bitcast.86, f32[8,512]{1,0:T(8,128)S(1)} %get-tuple-element.10, f32[8,128,128]{2,1,0:T(8,128)S(1)} %convolution_divide_fusion, f32[8,128]{1,0:T(8,128)S(1)} %bitcast.90, f32[128,128]{1,0:T(8,128)S(1)} %copy.41), kind=kOutput, calls=%fused_computation.11 | convolution fusion | flops 806748160 | bytes 3756032 | tf_op jit(solution)/shard_map/bjc,bjk->kbc/dot_general | solution.py:75
  70.3 0.7 copy.48
  71.5 1.4 %reduce.1 = bf16[128,4096]{0,1:T(8,128)(2,1)S(1)} reduce(bf16[128,1,4096]{0,2,1:T(8,128)(2,1)S(1)} %bitcast.87, bf16[]{:T(256)} %broadcast.60), dimensions={1}, to_apply=%copy.49.reduce_sub_computation | reduce | bytes 2097154 | tf_op jit(solution)/shard_map/reshape | solution.py:93
  73.4 0.7 reshape.79
  74.2 37.7 %all_to_all.24 = bf16[64,2,4096]{2,1,0:T(2,128)(2,1)S(1)} all-to-all(bf16[64,2,4096]{2,1,0:T(2,128)(2,1)S(1)} %reshape.79), channel_id=1, replica_groups=mesh['mem'=64,'blk'=4] {'mem'}, dimensions={0} | all-to-all | bytes 2097152 | tf_op jit(solution)/shard_map/all_to_all | solution.py:94
  111.9 1.0 reshape.80
  112.9 6.4 %reduce = bf16[128,4096]{1,0:T(8,128)(2,1)S(1)} reduce(bf16[128,1,4096]{2,1,0:T(2,128)(2,1)S(1)} %reshape.80, bf16[]{:T(256)} %constant.24), dimensions={1}, to_apply=%all_to_all.9.reduce_sub_computation | reduce | bytes 2097154 | tf_op jit(solution)/shard_map/all_to_all | solution.py:94
  119.3 1.5 %all_to_all.20 = bf16[64,2,1,4096]{3,1,0,2:T(2,128)(2,1)} reshape(bf16[128,4096]{1,0:T(8,128)(2,1)S(1)} %reduce) | data formatting | bytes 2097152 | tf_op jit(solution)/shard_map/all_to_all | solution.py:94
  (33 shorter events, 6.8 us)
Async XLA Ops:
  2.5 41.5 %all-to-all-start = ((bf16[2,64,8,512]{3,2,0,1:T(8,128)(2,1)}), bf16[2,64,8,512]{3,2,0,1:T(8,128)(2,1)S(1)}, u32[]{:S(2)}, u32[]{:S(2)}) async-start(bf16[2,64,8,512]{3,2,0,1:T(8,128)(2,1)} %copy.42), calls=%async_computation | async-start | bytes 2097152 | tf_op jit(solution)/shard_map/all_to_all | solution.py:85
  44.4 1.2 copy-start.3
  44.4 3.4 %copy-start = (f32[1,8,256]{2,1,0:T(8,128)S(1)}, f32[1,8,256]{2,1,0:T(8,128)}, u32[]{:S(2)}) copy-start(f32[1,8,256]{2,1,0:T(8,128)} %param.8) | copy-start | bytes 24580
  44.4 3.4 %copy-start.1 = (f32[1,8,256]{2,1,0:T(8,128)S(1)}, f32[1,8,256]{2,1,0:T(8,128)}, u32[]{:S(2)}) copy-start(f32[1,8,256]{2,1,0:T(8,128)} %param.9) | copy-start | bytes 24580
  44.4 3.4 %copy-start.2 = (s32[1,8]{1,0:T(1,128)S(1)}, s32[1,8]{1,0:T(1,128)}, u32[]{:S(2)}) copy-start(s32[1,8]{1,0:T(1,128)} %param.7) | copy-start | bytes 100
  51.4 2.4 %collective-permute-start = (bf16[1,129,256]{2,1,0:T(8,128)(2,1)S(1)}, bf16[1,129,256]{2,1,0:T(8,128)(2,1)S(1)}, u32[]{:S(2)}, u32[]{:S(2)}) collective-permute-start(bf16[1,129,256]{2,1,0:T(8,128)(2,1)S(1)} %get-tuple-element.7), channel_id=1, source_target_pairs={{0,4},{4,8},{8,12},{12,16},{16,20},{20,24},{24,28},{28,32},{32,36}... | collective-permute-start | bytes 198152 | tf_op jit(solution)/shard_map/ppermute | solution.py:19
  52.4 3.7 %collective-permute-start.1 = (bf16[1,129,256]{2,1,0:T(8,128)(2,1)S(1)}, bf16[1,129,256]{2,1,0:T(8,128)(2,1)S(1)}, u32[]{:S(2)}, u32[]{:S(2)}) collective-permute-start(bf16[1,129,256]{2,1,0:T(8,128)(2,1)S(1)} %get-tuple-element.8), channel_id=1, source_target_pairs={{4,0},{8,4},{12,8},{16,12},{20,16},{24,20},{28,24},{32,28},{36,32}... | collective-permute-start | bytes 198152 | tf_op jit(solution)/shard_map/ppermute | solution.py:22
where the time goes:
time: 121 us
  blocking collectives  37.7 us (31%)
  waiting for transfers between devices  32 us (26%)
  matrix products  19.4 us (16%)
  starting transfers between devices  14 us (12%)
  other arithmetic  9.64 us (8%)
  local copies, waits for them, and re-layouts  7.71 us (6%)
    all_to_all x1, blocking collectives, on_device(): lax.all_to_all(outgoing, 'mem', split_axis=0, concat_axis=1, tiled=True)  37.7 us
    all_to_all x1, waiting for transfers between devices, on_device(): lax.all_to_all(pieces, 'mem', split_axis=1, concat_axis=0, tiled=True)  28.3 us
    all_to_all x1, starting transfers between devices, on_device(): lax.all_to_all(pieces, 'mem', split_axis=1, concat_axis=0, tiled=True)  13 us
    dot_general x11, matrix products, batch_mm(): jnp.einsum('bij,bjk->bik', left, right, precision=lax.Precision.HIGHEST)  8.15 us
    all_to_all x1, other arithmetic, on_device(): lax.all_to_all(outgoing, 'mem', split_axis=0, concat_axis=1, tiled=True)  6.38 us
    unnamed x12, local copies, waits for them, and re-layouts  3.72 us
    dot_general x1, matrix products, observe(): jnp.einsum('bkc,boc->bko', deviation, selector, precision=lax.Precision.H...  3.46 us
    dot_general x1, matrix products, transform_apply(): jnp.einsum('bjc,bjk->kbc', deviation, mixing, precision=lax.Precision.HIG...  3.4 us
  transfers between devices with their start and end apart: 3, of which 3 were waited for; matrix products, arithmetic and copies ran while one was open for 0% of the time, Pallas kernels for 0%

commit v1 on v0

v1 whole, which is shorter than its diff:
```python
import jax
import jax.numpy as jnp
from jax import lax
from jax.experimental import pallas as pl
from jax.experimental.pallas import tpu as pltpu
from jax.sharding import PartitionSpec as P

NS_ITERS = 4
localize = 0.5
inflation = 1.1

BF = jnp.bfloat16
F32 = jnp.float32
ROWS = 144


def split(a):
    high = a.astype(BF)
    return high, (a - high.astype(F32)).astype(BF)


def left_of(a):
    return jnp.concatenate(split(a), axis=1)


def right_of(a):
    pair = jnp.concatenate(split(a), axis=1)
    return jnp.concatenate([pair, pair], axis=0)


def fold(wide):
    half = wide.shape[1] // 2
    return wide[:, :half] + wide[:, half:]


def dot(a, b):
    return jnp.dot(a, b, preferred_element_type=F32)


def mm(left, right):
    return fold(dot(left, right))


def members_of(x_ref, b, width):
    piece = x_ref[:, :, b * width : (b + 1) * width]
    return piece.reshape(piece.shape[0] * piece.shape[1], width)


def centre(members):
    values = members.astype(F32)
    return values, jnp.sum(values, axis=0, keepdims=True) * (1.0 / members.shape[0])


def rows_of(members, average, cells, count, obs_value, obs_rinv):
    width, slots = members.shape[1], cells.shape[1]
    high = average.astype(BF).astype(F32)
    rest = average - high
    middle = rest.astype(BF).astype(F32)
    low = rest - middle
    line = lax.broadcasted_iota(jnp.int32, (16, width), 0)
    pieces = jnp.where(line == 0, high, jnp.where(line == 1, middle, jnp.where(line == 2, low, 0.0)))
    stacked = jnp.concatenate([members, pieces.astype(BF)], axis=0)
    position = lax.broadcasted_iota(jnp.int32, (width, slots), 0)
    selector = jnp.where(position == cells, 1.0, 0.0).astype(BF)
    sampled = dot(stacked, selector)
    size = members.shape[0]
    mean_at = jnp.sum(sampled[size:], axis=0, keepdims=True)
    slot = lax.broadcasted_iota(jnp.int32, (1, slots), 1)
    root = jnp.where(slot < count, jnp.sqrt(obs_rinv), 0.0)
    upper = (sampled[:size] - mean_at) * root
    lower = root * (obs_value - mean_at)
    line = lax.broadcasted_iota(jnp.int32, (ROWS - size, slots), 0)
    lower = jnp.where(line == 0, lower, 0.0)
    return jnp.concatenate([upper, lower], axis=0).astype(BF)


def gram_of(rows):
    return lax.dot_general(rows, rows[:128], (((1,), (1,)), ((), ())), preferred_element_type=F32)


def eye_of(size):
    i = lax.broadcasted_iota(jnp.int32, (size, size), 0)
    j = lax.broadcasted_iota(jnp.int32, (size, size), 1)
    return jnp.where(i == j, 1.0, 0.0).astype(F32)


def transforms(localized, eye):
    size = eye.shape[0]
    systems = [g[:size] + (size - 1) / inflation * eye for g in localized]
    forcings = [g[size : size + 1] for g in localized]
    bounds = [
        jnp.max(jnp.sum(jnp.abs(a), axis=0, keepdims=True), axis=1, keepdims=True) for a in systems
    ]
    scales = [1.0 / b for b in bounds]
    y = [a * s for a, s in zip(systems, scales)]
    u = [1.5 * eye - 0.5 * a for a in y]
    z = u
    y = [mm(left_of(a), right_of(b)) for a, b in zip(y, u)]
    for iteration in range(NS_ITERS - 1):
        u = [1.5 * eye - 0.5 * mm(left_of(a), right_of(b)) for a, b in zip(z, y)]
        if iteration < NS_ITERS - 2:
            both = [
                mm(jnp.concatenate([left_of(a), left_of(c)], axis=0), right_of(b))
                for a, c, b in zip(y, z, u)
            ]
            y = [a[:size] for a in both]
            z = [a[size:] for a in both]
        else:
            z = [mm(left_of(a), right_of(b)) for a, b in zip(z, u)]
    out = []
    for a, f, s in zip(z, forcings, scales):
        inner = jnp.sum(a * f, axis=1, keepdims=True)
        weights = jnp.sum(a * inner, axis=0, keepdims=True) * s
        out.append(jnp.sqrt(s * (size - 1.0)) * a + weights - eye)
    return out


def apply_to(transform, values, average):
    high, low = split(values - average)
    t_high, t_low = split(transform)
    increment = dot(jnp.concatenate([t_high, t_low], axis=1), jnp.concatenate([high, high], axis=0))
    return (increment + dot(t_high, low)).astype(BF)


def boundary_rows_kernel(blocks, x_ref, cell_ref, count_ref, value_ref, rinv_ref, first_ref, last_ref):
    width = x_ref.shape[2] // blocks
    for b, out_ref in ((0, first_ref), (blocks - 1, last_ref)):
        members = members_of(x_ref, b, width)
        _, average = centre(members)
        out_ref[...] = rows_of(
            members, average, cell_ref[b : b + 1], count_ref[0, b], value_ref[b : b + 1], rinv_ref[b : b + 1]
        )


def interior_kernel(
    blocks, x_ref, cell_ref, count_ref, value_ref, rinv_ref, first_ref, last_ref, out_ref, part_ref
):
    width = x_ref.shape[2] // blocks
    inner = range(1, blocks - 1)
    values, averages, grams = {}, {}, {}
    grams[0] = gram_of(first_ref[...])
    grams[blocks - 1] = gram_of(last_ref[...])
    for b in inner:
        members = members_of(x_ref, b, width)
        _, average = centre(members)
        grams[b] = gram_of(
            rows_of(members, average, cell_ref[b : b + 1], count_ref[0, b], value_ref[b : b + 1], rinv_ref[b : b + 1])
        )
    part_ref[0] = grams[0] + localize * grams[1]
    part_ref[1] = grams[blocks - 1] + localize * grams[blocks - 2]
    eye = eye_of(128)
    mixed = transforms([grams[b] + localize * (grams[b - 1] + grams[b + 1]) for b in inner], eye)
    for b, transform in zip(inner, mixed):
        values, average = centre(members_of(x_ref, b, width))
        result = apply_to(transform, values, average)
        out_ref[:, :, (b - 1) * width : b * width] = result.reshape(x_ref.shape[0], x_ref.shape[1], width)


def boundary_kernel(blocks, x_ref, part_ref, left_ref, right_ref, in_ref, out_ref):
    width = x_ref.shape[2] // blocks
    out_ref[:, :, width : (blocks - 1) * width] = in_ref[...]
    eye = eye_of(128)
    localized = [
        part_ref[0] + localize * gram_of(left_ref[...]),
        part_ref[1] + localize * gram_of(right_ref[...]),
    ]
    for b, transform in zip((0, blocks - 1), transforms(localized, eye)):
        values, average = centre(members_of(x_ref, b, width))
        result = apply_to(transform, values, average)
        out_ref[:, :, b * width : (b + 1) * width] = result.reshape(x_ref.shape[0], x_ref.shape[1], width)


VMEM = pl.BlockSpec(memory_space=pltpu.VMEM)
SMEM = pl.BlockSpec(memory_space=pltpu.SMEM)


def call(kernel, out_shape, args, specs, flops):
    outs = jax.tree.map(lambda _: VMEM, out_shape)
    moved = sum(a.size * a.dtype.itemsize for a in args)
    return pl.pallas_call(
        kernel,
        out_shape=out_shape,
        in_specs=specs,
        out_specs=outs,
        cost_estimate=pl.CostEstimate(flops=flops, bytes_accessed=moved, transcendentals=0),
        compiler_params=pltpu.CompilerParams(vmem_limit_bytes=40 * 2**20),
    )(*args)


def analyse(arrived, cells, counts, obs_value, obs_rinv, exchange):
    blocks, slots = cells.shape
    kernel = lambda body: (lambda *refs: body(blocks, *refs))
    rows = jax.ShapeDtypeStruct((ROWS, slots), BF)
    obs = (cells, counts, obs_value, obs_rinv)
    specs = [VMEM, VMEM, SMEM, VMEM, VMEM]
    first, last = call(kernel(boundary_rows_kernel), (rows, rows), (arrived,) + obs, specs, 2 * 10**8)
    left, right = exchange(first, last)
    part = jax.ShapeDtypeStruct((2, ROWS, 128), F32)
    out = jax.ShapeDtypeStruct(arrived.shape[:2] + (arrived.shape[2] // blocks * (blocks - 2),), BF)
    out, part = call(
        kernel(interior_kernel), (out, part), (arrived,) + obs + (first, last), specs + [VMEM, VMEM], 5 * 10**9
    )
    return call(
        kernel(boundary_kernel), jax.ShapeDtypeStruct(arrived.shape, BF), (arrived, part, left, right, out),
        [VMEM] * 5, 2 * 10**9,
    )


def neighbours(first, last):
    count = lax.axis_size("mem")
    forward = [(i, (i + 1) % count) for i in range(count)]
    backward = [(target, source) for source, target in forward]
    return lax.ppermute(last, "mem", forward), lax.ppermute(first, "mem", backward)


def on_device(ensemble, obs_cell, obs_count, obs_value, obs_rinv):
    groups = lax.axis_size("mem")
    local = ensemble.shape[0]
    pieces = ensemble.reshape(local, groups, -1).transpose(1, 0, 2)
    arrived = lax.all_to_all(pieces, "mem", split_axis=0, concat_axis=0, tiled=True)
    outgoing = analyse(arrived, obs_cell[0], obs_count, obs_value[0], obs_rinv[0], neighbours)
    returned = lax.all_to_all(outgoing, "mem", split_axis=0, concat_axis=0, tiled=True)
    return returned.transpose(1, 0, 2).reshape(ensemble.shape)


def solution(mesh):
    placed = (
        P("mem", "blk"),
        P("blk", "mem", None),
        P("blk", "mem"),
        P("blk", "mem", None),
        P("blk", "mem", None),
    )
    return jax.shard_map(
        on_device, mesh=mesh, in_specs=placed, out_specs=P("mem", "blk"), check_vma=False
    )
```

time: 121 us -> 89.8 us (0.74)
  blocking collectives: 37.7 us -> 77.2 us
  waiting for transfers between devices: 32 us -> 0.01 us
  matrix products: 19.4 us -> 0 us
  starting transfers between devices: 14 us -> 1.82 us
  other arithmetic: 9.64 us -> 0 us
  Pallas kernels: 0 us -> 8.85 us
  local copies, waits for them, and re-layouts: 7.71 us -> 1.63 us
    all_to_all x1 -> x2, blocking collectives: 37.7 us -> 77.2 us  [the longest x1 41.7 us: on_device(): lax.all_to_all(pieces, 'mem', split_axis=0, concat_axis=0, tiled=True)]
    all_to_all x1 -> x0, waiting for transfers between devices: 28.3 us -> none  [on_device(): lax.all_to_all(pieces, 'mem', split_axis=1, concat_axis=0, tiled=True)]
    dot_general x17 -> x0, matrix products: 19.4 us -> none  [the longest x11 8.15 us: batch_mm(): jnp.einsum('bij,bjk->bik', left, right, precision=lax.Precision.HIGHEST)]
    all_to_all x1 -> x0, starting transfers between devices: 13 us -> none  [on_device(): lax.all_to_all(pieces, 'mem', split_axis=1, concat_axis=0, tiled=True)]
    pallas_call x0 -> x3, Pallas kernels: none -> 8.85 us  [call(): pl.pallas_call(kernel, out_shape=out_shape, in_specs=specs, out_specs=out...]
    all_to_all x1 -> x0, other arithmetic: 6.38 us -> none  [on_device(): lax.all_to_all(outgoing, 'mem', split_axis=0, concat_axis=1, tiled=True)]
    ppermute x2, waiting for transfers between devices: 3.72 us -> 0.01 us  [the longest x1 0.01 us: neighbours(): lax.ppermute(last, 'mem', forward)]
    unnamed x12 -> x9, local copies, waits for them, and re-layouts: 3.72 us -> 1.63 us
  transfers between devices with their start and end apart: 3 -> 2, of which waited for: 3 -> 0; matrix products, arithmetic and copies ran while one was open for 0% -> 0% of each run, Pallas kernels for 0% -> 6%
where the time goes in v1:
time: 89.8 us; the launch traced here: 89.6 us
  blocking collectives  77.2 us (86%)
  Pallas kernels  8.85 us (10%)
  starting transfers between devices  1.82 us (2%)
  local copies, waits for them, and re-layouts  1.63 us (2%)
    all_to_all x1, blocking collectives, on_device(): lax.all_to_all(pieces, 'mem', split_axis=0, concat_axis=0, tiled=True)  41.7 us
    all_to_all x1, blocking collectives, on_device(): lax.all_to_all(outgoing, 'mem', split_axis=0, concat_axis=0, tiled=True)  35.5 us
    pallas_call x3, Pallas kernels, call(): pl.pallas_call(kernel, out_shape=out_shape, in_specs=specs, out_specs=out...  8.85 us
  transfers between devices with their start and end apart: 2, of which 0 were waited for; matrix products, arithmetic and copies ran while one was open for 0% of the time, Pallas kernels for 6%

profile of v1, /device:TPU:1, one launch (start us, length us, event | category | flops | bytes accessed | tf_op | source)
XLA Modules:
  0.0 89.6 jit_solution(8771004467129273034)
XLA Ops:
  0.0 0.0 copy-start
  0.0 0.0 copy-start.1
  0.0 0.0 copy-start.2
  0.0 41.7 %all_to_all.10.refs_0_ = bf16[64,2,4096]{2,1,0:T(2,128)(2,1)S(1)} all-to-all(bf16[64,2,4096]{2,1,0:T(2,128)(2,1)} %bitcast.16), channel_id=1, replica_groups=mesh['mem'=64,'blk'=4] {'mem'}, dimensions={0} | all-to-all | bytes 2097152 | tf_op jit(solution)/shard_map/all_to_all | solution.py:220
  41.7 0.0 copy-start.3
  41.7 0.0 copy-done
  41.7 0.0 copy-done.1
  41.7 0.0 copy-done.2
  41.7 0.6 copy-done.3
  42.3 0.9 %shard_map.55 = (bf16[144,256]{1,0:T(8,128)(2,1)S(1)}, bf16[144,256]{1,0:T(8,128)(2,1)S(1)}) custom-call(bf16[64,2,4096]{2,1,0:T(2,128)(2,1)S(1)} %all_to_all.10.refs_0_, s32[8,256]{1,0:T(8,128)S(1)} %bitcast.9, s32[1,8]{1,0:T(1,128)S(1)} %copy-done.3, f32[8,256]{1,0:T(8,128)S(1)} %bitcast.11, f32[8,256]{1,0:T(8,128)S(1)} %bitcast.13), custom_call_target="tpu_custom_call" | custom-call | flops 200000000 | bytes 1073184 | tf_op jit(solution)/shard_map/pallas_call | solution.py:180
  43.3 0.2 collective-permute-start.1
  43.5 1.7 %collective-permute-start = (bf16[144,256]{1,0:T(8,128)(2,1)S(1)}, bf16[144,256]{1,0:T(8,128)(2,1)S(1)}, u32[]{:S(2)}, u32[]{:S(2)}) collective-permute-start(bf16[144,256]{1,0:T(8,128)(2,1)S(1)} %get-tuple-element.10.refs_6_), channel_id=1, source_target_pairs={{0,4},{4,8},{8,12},{12,16},{16,20},{20,24},{24,28},{28,32},{32,36}... | collective-permute-start | bytes 221192 | tf_op jit(solution)/shard_map/ppermute | solution.py:213
  45.1 5.6 %shard_map.56 = (bf16[64,2,3072]{2,1,0:T(2,128)(2,1)S(1)}, f32[2,144,128]{2,1,0:T(8,128)S(1)}) custom-call(bf16[64,2,4096]{2,1,0:T(2,128)(2,1)S(1)} %all_to_all.10.refs_0_, s32[8,256]{1,0:T(8,128)S(1)} %bitcast.10, s32[1,8]{1,0:T(1,128)S(1)} %copy-done.3, f32[8,256]{1,0:T(8,128)S(1)} %bitcast.12, f32[8,256]{1,0:T(8,128)S(1)} %bitcast.14, ...), custom_call_target="tpu_custom_call" | custom-call | flops 5000000000 | bytes 1220640 | tf_op jit(solution)/shard_map/pallas_call | solution.py:180
  50.8 0.0 collective-permute-done.1.refs_3_
  50.8 0.0 collective-permute-done.refs_2_
  50.8 2.3 %shard_map.57 = bf16[64,2,4096]{2,1,0:T(2,128)(2,1)S(1)} custom-call(bf16[64,2,4096]{2,1,0:T(2,128)(2,1)S(1)} %all_to_all.10.refs_0_, f32[2,144,128]{2,1,0:T(8,128)S(1)} %get-tuple-element.11.refs_1_, bf16[144,256]{1,0:T(8,128)(2,1)S(1)} %collective-permute-done.refs_2_, bf16[144,256]{1,0:T(8,128)(2,1)S(1)} %collective-permute-done.1.refs_3_, ...), custom_call_target="tpu_custom_call" | custom-call | flops 2000000000 | bytes 2129920 | tf_op jit(solution)/shard_map/pallas_call | solution.py:180
  53.1 35.5 %all_to_all.11 = bf16[64,2,4096]{2,1,0:T(2,128)(2,1)S(1)} all-to-all(bf16[64,2,4096]{2,1,0:T(2,128)(2,1)S(1)} %shard_map.57), channel_id=1, replica_groups=mesh['mem'=64,'blk'=4] {'mem'}, dimensions={0} | all-to-all | bytes 2097152 | tf_op jit(solution)/shard_map/all_to_all | solution.py:222
  88.6 1.0 %copy.7 = bf16[2,262144]{1,0:T(2,128)(2,1)} copy(bf16[2,262144]{1,0:T(2,128)(2,1)S(1)} %bitcast.15) | data formatting | bytes 2097152
Async XLA Ops:
  0.0 41.7 %copy-start = (s32[1,8,256]{2,1,0:T(8,128)S(1)}, s32[1,8,256]{2,1,0:T(8,128)}, u32[]{:S(2)}) copy-start(s32[1,8,256]{2,1,0:T(8,128)} %param.6) | copy-start | bytes 24580
  0.0 41.7 %copy-start.1 = (f32[1,8,256]{2,1,0:T(8,128)S(1)}, f32[1,8,256]{2,1,0:T(8,128)}, u32[]{:S(2)}) copy-start(f32[1,8,256]{2,1,0:T(8,128)} %param.8) | copy-start | bytes 24580
  0.0 41.7 %copy-start.2 = (f32[1,8,256]{2,1,0:T(8,128)S(1)}, f32[1,8,256]{2,1,0:T(8,128)}, u32[]{:S(2)}) copy-start(f32[1,8,256]{2,1,0:T(8,128)} %param.9) | copy-start | bytes 24580
  41.7 0.7 copy-start.3
  43.3 7.5 %collective-permute-start.1 = (bf16[144,256]{1,0:T(8,128)(2,1)S(1)}, bf16[144,256]{1,0:T(8,128)(2,1)S(1)}, u32[]{:S(2)}, u32[]{:S(2)}) collective-permute-start(bf16[144,256]{1,0:T(8,128)(2,1)S(1)} %get-tuple-element.9.refs_5_), channel_id=1, source_target_pairs={{4,0},{8,4},{12,8},{16,12},{20,16},{24,20},{28,24},{32,28},{36,32}... | collective-permute-start | bytes 221192 | tf_op jit(solution)/shard_map/ppermute | solution.py:213
  43.5 7.3 %collective-permute-start = (bf16[144,256]{1,0:T(8,128)(2,1)S(1)}, bf16[144,256]{1,0:T(8,128)(2,1)S(1)}, u32[]{:S(2)}, u32[]{:S(2)}) collective-permute-start(bf16[144,256]{1,0:T(8,128)(2,1)S(1)} %get-tuple-element.10.refs_6_), channel_id=1, source_target_pairs={{0,4},{4,8},{8,12},{12,16},{16,20},{20,24},{24,28},{28,32},{32,36}... | collective-permute-start | bytes 221192 | tf_op jit(solution)/shard_map/ppermute | solution.py:213

commit v2 on v1

--- a/solution.py
+++ b/solution.py
@@ -115,72 +115,72 @@
     return out
 
 
-def apply_to(transform, values, average):
-    high, low = split(values - average)
-    t_high, t_low = split(transform)
-    increment = dot(jnp.concatenate([t_high, t_low], axis=1), jnp.concatenate([high, high], axis=0))
-    return (increment + dot(t_high, low)).astype(BF)
-
-
-def boundary_rows_kernel(blocks, x_ref, cell_ref, count_ref, value_ref, rinv_ref, first_ref, last_ref):
+def apply_to(transform, deviation):
+    high, low = split(transform)
+    increment = dot(jnp.concatenate([high, high], axis=1), deviation)
+    return (increment + dot(low, deviation[:128])).astype(BF)
+
+
+def block_rows(b, members, average, obs_refs):
+    cell_ref, count_ref, value_ref, rinv_ref = obs_refs
+    one = slice(b, b + 1)
+    return rows_of(members, average, cell_ref[one], count_ref[0:1, one], value_ref[one], rinv_ref[one])
+
+
+def boundary_kernel(blocks, x_ref, cell_ref, count_ref, value_ref, rinv_ref, first_ref, last_ref):
     width = x_ref.shape[2] // blocks
     for b, out_ref in ((0, first_ref), (blocks - 1, last_ref)):
         members = members_of(x_ref, b, width)
         _, average = centre(members)
-        out_ref[...] = rows_of(
-            members, average, cell_ref[b : b + 1], count_ref[0, b], value_ref[b : b + 1], rinv_ref[b : b + 1]
-        )
-
-
-def interior_kernel(
-    blocks, x_ref, cell_ref, count_ref, value_ref, rinv_ref, first_ref, last_ref, out_ref, part_ref
+        out_ref[...] = block_rows(b, members, average, (cell_ref, count_ref, value_ref, rinv_ref))
+
+
+def gram_kernel(
+    blocks, x_ref, cell_ref, count_ref, value_ref, rinv_ref, first_ref, last_ref, local_ref, dev_ref
 ):
     width = x_ref.shape[2] // blocks
-    inner = range(1, blocks - 1)
-    values, averages, grams = {}, {}, {}
-    grams[0] = gram_of(first_ref[...])
-    grams[blocks - 1] = gram_of(last_ref[...])
-    for b in inner:
+    grams = []
+    for b in range(blocks):
         members = members_of(x_ref, b, width)
-        _, average = centre(members)
-        grams[b] = gram_of(
-            rows_of(members, average, cell_ref[b : b + 1], count_ref[0, b], value_ref[b : b + 1], rinv_ref[b : b + 1])
-        )
-    part_ref[0] = grams[0] + localize * grams[1]
-    part_ref[1] = grams[blocks - 1] + localize * grams[blocks - 2]
-    eye = eye_of(128)
-    mixed = transforms([grams[b] + localize * (grams[b - 1] + grams[b + 1]) for b in inner], eye)
-    for b, transform in zip(inner, mixed):
-        values, average = centre(members_of(x_ref, b, width))
-        result = apply_to(transform, values, average)
-        out_ref[:, :, (b - 1) * width : b * width] = result.reshape(x_ref.shape[0], x_ref.shape[1], width)
-
-
-def boundary_kernel(blocks, x_ref, part_ref, left_ref, right_ref, in_ref, out_ref):
-    width = x_ref.shape[2] // blocks
-    out_ref[:, :, width : (blocks - 1) * width] = in_ref[...]
-    eye = eye_of(128)
-    localized = [
-        part_ref[0] + localize * gram_of(left_ref[...]),
-        part_ref[1] + localize * gram_of(right_ref[...]),
-    ]
-    for b, transform in zip((0, blocks - 1), transforms(localized, eye)):
-        values, average = centre(members_of(x_ref, b, width))
-        result = apply_to(transform, values, average)
-        out_ref[:, :, b * width : (b + 1) * width] = result.reshape(x_ref.shape[0], x_ref.shape[1], width)
+        values, average = centre(members)
+        high, low = split(values - average)
+        dev_ref[b, :128] = high
+        dev_ref[b, 128:] = low
+        if b == 0:
+            rows = first_ref[...]
+        elif b == blocks - 1:
+            rows = last_ref[...]
+        else:
+            rows = block_rows(b, members, average, (cell_ref, count_ref, value_ref, rinv_ref))
+        grams.append(gram_of(rows))
+        if b > 0:
+            below = grams[b - 1]
+            if b > 1:
+                below = below + localize * grams[b - 2]
+            local_ref[b - 1] = below + localize * grams[b]
+    local_ref[blocks - 1] = grams[blocks - 1] + localize * grams[blocks - 2]
+
+
+def analysis_kernel(blocks, local_ref, dev_ref, left_ref, right_ref, out_ref):
+    width = out_ref.shape[2] // blocks
+    localized = [local_ref[b] for b in range(blocks)]
+    localized[0] = localized[0] + localize * gram_of(left_ref[...])
+    localized[-1] = localized[-1] + localize * gram_of(right_ref[...])
+    for b, transform in enumerate(transforms(localized, eye_of(128))):
+        result = apply_to(transform, dev_ref[b])
+        out_ref[:, :, b * width : (b + 1) * width] = result.reshape(out_ref.shape[0], out_ref.shape[1], width)
 
 
 VMEM = pl.BlockSpec(memory_space=pltpu.VMEM)
-SMEM = pl.BlockSpec(memory_space=pltpu.SMEM)
-
-
-def call(kernel, out_shape, args, specs, flops):
+
+
+def call(kernel, out_shape, args, flops):
     outs = jax.tree.map(lambda _: VMEM, out_shape)
     moved = sum(a.size * a.dtype.itemsize for a in args)
     return pl.pallas_call(
         kernel,
         out_shape=out_shape,
-        in_specs=specs,
+        in_specs=[VMEM] * len(args),
         out_specs=outs,
         cost_estimate=pl.CostEstimate(flops=flops, bytes_accessed=moved, transcendentals=0),
         compiler_params=pltpu.CompilerParams(vmem_limit_bytes=40 * 2**20),
@@ -192,17 +192,15 @@
     kernel = lambda body: (lambda *refs: body(blocks, *refs))
     rows = jax.ShapeDtypeStruct((ROWS, slots), BF)
     obs = (cells, counts, obs_value, obs_rinv)
-    specs = [VMEM, VMEM, SMEM, VMEM, VMEM]
-    first, last = call(kernel(boundary_rows_kernel), (rows, rows), (arrived,) + obs, specs, 2 * 10**8)
+    first, last = call(kernel(boundary_kernel), (rows, rows), (arrived,) + obs, 2 * 10**8)
     left, right = exchange(first, last)
-    part = jax.ShapeDtypeStruct((2, ROWS, 128), F32)
-    out = jax.ShapeDtypeStruct(arrived.shape[:2] + (arrived.shape[2] // blocks * (blocks - 2),), BF)
-    out, part = call(
-        kernel(interior_kernel), (out, part), (arrived,) + obs + (first, last), specs + [VMEM, VMEM], 5 * 10**9
+    localized = jax.ShapeDtypeStruct((blocks, ROWS, 128), F32)
+    deviation = jax.ShapeDtypeStruct((blocks, 256, arrived.shape[2] // blocks), BF)
+    localized, deviation = call(
+        kernel(gram_kernel), (localized, deviation), (arrived,) + obs + (first, last), 5 * 10**9
     )
     return call(
-        kernel(boundary_kernel), jax.ShapeDtypeStruct(arrived.shape, BF), (arrived, part, left, right, out),
-        [VMEM] * 5, 2 * 10**9,
+        kernel(analysis_kernel), jax.ShapeDtypeStruct(arrived.shape, BF), (localized, deviation, left, right), 5 * 10**9
     )
 
 
@@ -215,12 +213,12 @@
 
 def on_device(ensemble, obs_cell, obs_count, obs_value, obs_rinv):
     groups = lax.axis_size("mem")
-    local = ensemble.shape[0]
-    pieces = ensemble.reshape(local, groups, -1).transpose(1, 0, 2)
-    arrived = lax.all_to_all(pieces, "mem", split_axis=0, concat_axis=0, tiled=True)
+    local, cells = ensemble.shape
+    arrived = lax.all_to_all(ensemble, "mem", split_axis=1, concat_axis=1, tiled=True)
+    arrived = arrived.reshape(local, groups, cells // groups).transpose(1, 0, 2)
     outgoing = analyse(arrived, obs_cell[0], obs_count, obs_value[0], obs_rinv[0], neighbours)
-    returned = lax.all_to_all(outgoing, "mem", split_axis=0, concat_axis=0, tiled=True)
-    return returned.transpose(1, 0, 2).reshape(ensemble.shape)
+    outgoing = outgoing.transpose(1, 0, 2).reshape(local, cells)
+    return lax.all_to_all(outgoing, "mem", split_axis=1, concat_axis=1, tiled=True)
 
 
 def solution(mesh):

time: 89.8 us -> 88.6 us (0.987)
  Pallas kernels: 8.85 us -> 5.93 us
  blocking collectives: 77.2 us -> 79.4 us
  waiting for transfers between devices: 0.01 us -> 0.94 us
    pallas_call x3, Pallas kernels: 8.85 us -> 5.93 us  [call(): pl.pallas_call(kernel, out_shape=out_shape, in_specs=[VMEM] * len(args),...]
    all_to_all x2, blocking collectives: 77.2 us -> 79.4 us  [the longest x1 41.7 us: on_device(): lax.all_to_all(ensemble, 'mem', split_axis=1, concat_axis=1, tiled=True)]
    ppermute x1, waiting for transfers between devices: 0.01 us -> 0.94 us  [neighbours(): lax.ppermute(first, 'mem', backward)]
  transfers between devices with their start and end apart: 2 -> 2, of which waited for: 0 -> 1; matrix products, arithmetic and copies ran while one was open for 0% -> 0% of each run, Pallas kernels for 6% -> 3%
where the time goes in v2:
time: 88.6 us; the launch traced here: 88.3 us
  blocking collectives  79.4 us (90%)
  Pallas kernels  5.93 us (7%)
  starting transfers between devices  1.03 us (1%)
  local copies, waits for them, and re-layouts  0.99 us (1%)
  waiting for transfers between devices  0.94 us (1%)
    all_to_all x1, blocking collectives, on_device(): lax.all_to_all(ensemble, 'mem', split_axis=1, concat_axis=1, tiled=True)  41.7 us
    all_to_all x1, blocking collectives, on_device(): lax.all_to_all(outgoing, 'mem', split_axis=1, concat_axis=1, tiled=True)  37.7 us
    pallas_call x3, Pallas kernels, call(): pl.pallas_call(kernel, out_shape=out_shape, in_specs=[VMEM] * len(args),...  5.93 us
  transfers between devices with their start and end apart: 2, of which 1 were waited for; matrix products, arithmetic and copies ran while one was open for 0% of the time, Pallas kernels for 3%

profile of v2, /device:TPU:1, one launch (start us, length us, event | category | flops | bytes accessed | tf_op | source)
XLA Modules:
  0.0 88.3 jit_solution(7190442922254296473)
XLA Ops:
  0.0 0.0 copy-start
  0.0 0.0 copy-start.1
  0.0 0.0 copy-start.2
  0.0 0.0 copy-start.3
  0.0 41.7 %all_to_all.18 = bf16[2,64,4096]{2,0,1:T(2,128)(2,1)S(1)} all-to-all(bf16[2,64,4096]{2,0,1:T(2,128)(2,1)} %bitcast.17), channel_id=1, replica_groups=mesh['mem'=64,'blk'=4] {'mem'}, dimensions={1} | all-to-all | bytes 2097152 | tf_op jit(solution)/shard_map/all_to_all | solution.py:217
  41.7 0.0 copy-done
  41.7 0.0 copy-done.1
  41.7 0.0 copy-done.2
  41.7 0.0 copy-done.3
  41.7 0.4 shard_map.55
  42.1 1.0 %collective-permute-start = (bf16[144,256]{1,0:T(8,128)(2,1)S(1)}, bf16[144,256]{1,0:T(8,128)(2,1)S(1)}, u32[]{:S(2)}, u32[]{:S(2)}) collective-permute-start(bf16[144,256]{1,0:T(8,128)(2,1)S(1)} %get-tuple-element.10.refs_6_), channel_id=1, source_target_pairs={{0,4},{4,8},{8,12},{12,16},{16,20},{20,24},{24,28},{28,32},{32,36}... | collective-permute-start | bytes 221192 | tf_op jit(solution)/shard_map/ppermute | solution.py:211
  43.2 0.0 collective-permute-start.1
  43.2 2.8 %shard_map.56 = (f32[8,144,128]{2,1,0:T(8,128)S(1)}, bf16[8,256,512]{2,1,0:T(8,128)(2,1)S(1)}) custom-call(bf16[64,2,4096]{2,1,0:T(2,128)(2,1)S(1)} %bitcast.8, s32[8,256]{1,0:T(8,128)S(1)} %bitcast.11, s32[1,8]{1,0:T(1,128)S(1)} %copy-done.3, f32[8,256]{1,0:T(8,128)S(1)} %bitcast.13, f32[8,256]{1,0:T(8,128)S(1)} %bitcast.15, ...), custom_call_target="tpu_custom_call" | custom-call | flops 5000000000 | bytes 1220640 | tf_op jit(solution)/shard_map/pallas_call | solution.py:180
  46.0 0.0 collective-permute-done.refs_2_
  46.0 0.9 %collective-permute-done.1.refs_3_ = bf16[144,256]{1,0:T(8,128)(2,1)S(1)} collective-permute-done((bf16[144,256]{1,0:T(8,128)(2,1)S(1)}, bf16[144,256]{1,0:T(8,128)(2,1)S(1)}, u32[]{:S(2)}, u32[]{:S(2)}) %collective-permute-start.1) | collective-permute-done | bytes 73760 | tf_op jit(solution)/shard_map/ppermute | solution.py:211
  46.9 2.7 %shard_map.57 = bf16[64,2,4096]{2,1,0:T(2,128)(2,1)S(1)} custom-call(f32[8,144,128]{2,1,0:T(8,128)S(1)} %get-tuple-element.11.refs_0_, bf16[8,256,512]{2,1,0:T(8,128)(2,1)S(1)} %get-tuple-element.12.refs_1_, bf16[144,256]{1,0:T(8,128)(2,1)S(1)} %collective-permute-done.refs_2_, bf16[144,256]{1,0:T(8,128)(2,1)S(1)} %collective-permute-done.1.refs_3_), custom_call_target="tpu_custom_call" | custom-call | flops 5000000000 | bytes 2834432 | tf_op jit(solution)/shard_map/pallas_call | solution.py:180
  49.7 37.7 %all_to_all.19 = bf16[2,64,4096]{2,0,1:T(2,128)(2,1)S(1)} all-to-all(bf16[2,64,4096]{2,0,1:T(2,128)(2,1)S(1)} %bitcast.9), channel_id=1, replica_groups=mesh['mem'=64,'blk'=4] {'mem'}, dimensions={1} | all-to-all | bytes 2097152 | tf_op jit(solution)/shard_map/all_to_all | solution.py:221
  87.3 1.0 %copy.7 = bf16[2,262144]{1,0:T(2,128)(2,1)} copy(bf16[2,262144]{1,0:T(2,128)(2,1)S(1)} %bitcast.16) | data formatting | bytes 2097152
Async XLA Ops:
  0.0 41.7 %copy-start = (s32[1,8,256]{2,1,0:T(8,128)S(1)}, s32[1,8,256]{2,1,0:T(8,128)}, u32[]{:S(2)}) copy-start(s32[1,8,256]{2,1,0:T(8,128)} %param.6) | copy-start | bytes 24580
  0.0 41.7 %copy-start.1 = (f32[1,8,256]{2,1,0:T(8,128)S(1)}, f32[1,8,256]{2,1,0:T(8,128)}, u32[]{:S(2)}) copy-start(f32[1,8,256]{2,1,0:T(8,128)} %param.8) | copy-start | bytes 24580
  0.0 41.7 %copy-start.2 = (f32[1,8,256]{2,1,0:T(8,128)S(1)}, f32[1,8,256]{2,1,0:T(8,128)}, u32[]{:S(2)}) copy-start(f32[1,8,256]{2,1,0:T(8,128)} %param.9) | copy-start | bytes 24580
  0.0 41.7 %copy-start.3 = (s32[1,8]{1,0:T(1,128)S(1)}, s32[1,8]{1,0:T(1,128)}, u32[]{:S(2)}) copy-start(s32[1,8]{1,0:T(1,128)} %refs_2_.3) | copy-start | bytes 100
  42.1 3.9 %collective-permute-start = (bf16[144,256]{1,0:T(8,128)(2,1)S(1)}, bf16[144,256]{1,0:T(8,128)(2,1)S(1)}, u32[]{:S(2)}, u32[]{:S(2)}) collective-permute-start(bf16[144,256]{1,0:T(8,128)(2,1)S(1)} %get-tuple-element.10.refs_6_), channel_id=1, source_target_pairs={{0,4},{4,8},{8,12},{12,16},{16,20},{20,24},{24,28},{28,32},{32,36}... | collective-permute-start | bytes 221192 | tf_op jit(solution)/shard_map/ppermute | solution.py:211
  43.2 3.8 %collective-permute-start.1 = (bf16[144,256]{1,0:T(8,128)(2,1)S(1)}, bf16[144,256]{1,0:T(8,128)(2,1)S(1)}, u32[]{:S(2)}, u32[]{:S(2)}) collective-permute-start(bf16[144,256]{1,0:T(8,128)(2,1)S(1)} %get-tuple-element.9.refs_5_), channel_id=1, source_target_pairs={{4,0},{8,4},{12,8},{16,12},{20,16},{24,20},{28,24},{32,28},{36,32}... | collective-permute-start | bytes 221192 | tf_op jit(solution)/shard_map/ppermute | solution.py:211

commit v3 on v2

--- a/solution.py
+++ b/solution.py
@@ -127,18 +127,41 @@
     return rows_of(members, average, cell_ref[one], count_ref[0:1, one], value_ref[one], rinv_ref[one])
 
 
-def boundary_kernel(blocks, x_ref, cell_ref, count_ref, value_ref, rinv_ref, first_ref, last_ref):
+def is_even():
+    return lax.rem(lax.axis_index("mem"), 2) == 0
+
+
+def boundary_kernel(blocks, x_ref, cell_ref, count_ref, value_ref, rinv_ref, across_ref, partner_ref):
     width = x_ref.shape[2] // blocks
-    for b, out_ref in ((0, first_ref), (blocks - 1, last_ref)):
+    rows = []
+    for b in (0, blocks - 1):
         members = members_of(x_ref, b, width)
         _, average = centre(members)
-        out_ref[...] = block_rows(b, members, average, (cell_ref, count_ref, value_ref, rinv_ref))
+        rows.append(block_rows(b, members, average, (cell_ref, count_ref, value_ref, rinv_ref)))
+    first, last = rows
+
+    @pl.when(is_even())
+    def _():
+        across_ref[...] = first
+        partner_ref[...] = last
+
+    @pl.when(jnp.logical_not(is_even()))
+    def _():
+        across_ref[...] = last
+        partner_ref[...] = first
+
+
+def ordered(across_ref, partner_ref):
+    across, partner = gram_of(across_ref[...]), gram_of(partner_ref[...])
+    even = is_even()
+    return jnp.where(even, across, partner), jnp.where(even, partner, across)
 
 
 def gram_kernel(
-    blocks, x_ref, cell_ref, count_ref, value_ref, rinv_ref, first_ref, last_ref, local_ref, dev_ref
+    blocks, x_ref, cell_ref, count_ref, value_ref, rinv_ref, across_ref, partner_ref, local_ref, dev_ref
 ):
     width = x_ref.shape[2] // blocks
+    first_gram, last_gram = ordered(across_ref, partner_ref)
     grams = []
     for b in range(blocks):
         members = members_of(x_ref, b, width)
@@ -147,12 +170,11 @@
         dev_ref[b, :128] = high
         dev_ref[b, 128:] = low
         if b == 0:
-            rows = first_ref[...]
+            grams.append(first_gram)
         elif b == blocks - 1:
-            rows = last_ref[...]
+            grams.append(last_gram)
         else:
-            rows = block_rows(b, members, average, (cell_ref, count_ref, value_ref, rinv_ref))
-        grams.append(gram_of(rows))
+            grams.append(gram_of(block_rows(b, members, average, (cell_ref, count_ref, value_ref, rinv_ref))))
         if b > 0:
             below = grams[b - 1]
             if b > 1:
@@ -161,11 +183,12 @@
     local_ref[blocks - 1] = grams[blocks - 1] + localize * grams[blocks - 2]
 
 
-def analysis_kernel(blocks, local_ref, dev_ref, left_ref, right_ref, out_ref):
+def analysis_kernel(blocks, local_ref, dev_ref, across_ref, partner_ref, out_ref):
     width = out_ref.shape[2] // blocks
     localized = [local_ref[b] for b in range(blocks)]
-    localized[0] = localized[0] + localize * gram_of(left_ref[...])
-    localized[-1] = localized[-1] + localize * gram_of(right_ref[...])
+    left, right = ordered(across_ref, partner_ref)
+    localized[0] = localized[0] + localize * left
+    localized[-1] = localized[-1] + localize * right
     for b, transform in enumerate(transforms(localized, eye_of(128))):
         result = apply_to(transform, dev_ref[b])
         out_ref[:, :, b * width : (b + 1) * width] = result.reshape(out_ref.shape[0], out_ref.shape[1], width)
@@ -192,23 +215,24 @@
     kernel = lambda body: (lambda *refs: body(blocks, *refs))
     rows = jax.ShapeDtypeStruct((ROWS, slots), BF)
     obs = (cells, counts, obs_value, obs_rinv)
-    first, last = call(kernel(boundary_kernel), (rows, rows), (arrived,) + obs, 2 * 10**8)
-    left, right = exchange(first, last)
+    across, partner = call(kernel(boundary_kernel), (rows, rows), (arrived,) + obs, 2 * 10**8)
+    halo = exchange(across, partner)
     localized = jax.ShapeDtypeStruct((blocks, ROWS, 128), F32)
     deviation = jax.ShapeDtypeStruct((blocks, 256, arrived.shape[2] // blocks), BF)
     localized, deviation = call(
-        kernel(gram_kernel), (localized, deviation), (arrived,) + obs + (first, last), 5 * 10**9
+        kernel(gram_kernel), (localized, deviation), (arrived,) + obs + (across, partner), 5 * 10**9
     )
     return call(
-        kernel(analysis_kernel), jax.ShapeDtypeStruct(arrived.shape, BF), (localized, deviation, left, right), 5 * 10**9
-    )
-
-
-def neighbours(first, last):
+        kernel(analysis_kernel), jax.ShapeDtypeStruct(arrived.shape, BF), (localized, deviation) + halo, 5 * 10**9
+    )
+
+
+def swap_boundaries(across, partner):
     count = lax.axis_size("mem")
-    forward = [(i, (i + 1) % count) for i in range(count)]
-    backward = [(target, source) for source, target in forward]
-    return lax.ppermute(last, "mem", forward), lax.ppermute(first, "mem", backward)
+    hops = [(i, (i + 1) % count) for i in range(1, count, 2)]
+    cores = [(i, i + 1) for i in range(0, count, 2)]
+    both_ways = lambda pairs: pairs + [(target, source) for source, target in pairs]
+    return lax.ppermute(across, "mem", both_ways(hops)), lax.ppermute(partner, "mem", both_ways(cores))
 
 
 def on_device(ensemble, obs_cell, obs_count, obs_value, obs_rinv):
@@ -216,7 +240,7 @@
     local, cells = ensemble.shape
     arrived = lax.all_to_all(ensemble, "mem", split_axis=1, concat_axis=1, tiled=True)
     arrived = arrived.reshape(local, groups, cells // groups).transpose(1, 0, 2)
-    outgoing = analyse(arrived, obs_cell[0], obs_count, obs_value[0], obs_rinv[0], neighbours)
+    outgoing = analyse(arrived, obs_cell[0], obs_count, obs_value[0], obs_rinv[0], swap_boundaries)
     outgoing = outgoing.transpose(1, 0, 2).reshape(local, cells)
     return lax.all_to_all(outgoing, "mem", split_axis=1, concat_axis=1, tiled=True)
 

time: 88.6 us -> 85.6 us (0.966)
  blocking collectives: 79.4 us -> 76.1 us
  starting transfers between devices: 1.03 us -> 2.12 us
  waiting for transfers between devices: 0.94 us -> 0.01 us
    all_to_all x1, blocking collectives: 37.7 us -> 34.4 us  [on_device(): lax.all_to_all(outgoing, 'mem', split_axis=1, concat_axis=1, tiled=True)]
    ppermute x2, starting transfers between devices: 1.03 us -> 2.12 us  [the longest x1 1.08 us: swap_boundaries(): lax.ppermute(partner, 'mem', both_ways(cores))]
    ppermute x2, waiting for transfers between devices: 0.94 us -> 0.01 us  [the longest x1 0.01 us: swap_boundaries(): lax.ppermute(partner, 'mem', both_ways(cores))]
  transfers between devices with their start and end apart: 2 -> 2, of which waited for: 1 -> 0; matrix products, arithmetic and copies ran while one was open for 0% -> 0% of each run, Pallas kernels for 3% -> 4%
where the time goes in v3:
time: 85.6 us; the launch traced here: 85.4 us
  blocking collectives  76.1 us (89%)
  Pallas kernels  6.14 us (7%)
  starting transfers between devices  2.12 us (2%)
  local copies, waits for them, and re-layouts  0.99 us (1%)
    all_to_all x1, blocking collectives, on_device(): lax.all_to_all(ensemble, 'mem', split_axis=1, concat_axis=1, tiled=True)  41.7 us
    all_to_all x1, blocking collectives, on_device(): lax.all_to_all(outgoing, 'mem', split_axis=1, concat_axis=1, tiled=True)  34.4 us
    pallas_call x3, Pallas kernels, call(): pl.pallas_call(kernel, out_shape=out_shape, in_specs=[VMEM] * len(args),...  6.14 us
  transfers between devices with their start and end apart: 2, of which 0 were waited for; matrix products, arithmetic and copies ran while one was open for 0% of the time, Pallas kernels for 4%

profile of v3, /device:TPU:1, one launch (start us, length us, event | category | flops | bytes accessed | tf_op | source)
XLA Modules:
  0.0 85.4 jit_solution(3553996691981139256)
XLA Ops:
  0.0 0.0 copy-start
  0.0 0.0 copy-start.1
  0.0 0.0 copy-start.2
  0.0 0.0 copy-start.3
  0.0 41.7 %all_to_all.18 = bf16[2,64,4096]{2,0,1:T(2,128)(2,1)S(1)} all-to-all(bf16[2,64,4096]{2,0,1:T(2,128)(2,1)} %bitcast.17), channel_id=1, replica_groups=mesh['mem'=64,'blk'=4] {'mem'}, dimensions={1} | all-to-all | bytes 2097152 | tf_op jit(solution)/shard_map/all_to_all | solution.py:241
  41.7 0.0 copy-done
  41.7 0.0 copy-done.1
  41.7 0.0 copy-done.2
  41.7 0.0 copy-done.3
  41.7 0.4 shard_map.55
  42.1 1.0 %collective-permute-start = (bf16[144,256]{1,0:T(8,128)(2,1)S(1)}, bf16[144,256]{1,0:T(8,128)(2,1)S(1)}, u32[]{:S(2)}, u32[]{:S(2)}) collective-permute-start(bf16[144,256]{1,0:T(8,128)(2,1)S(1)} %get-tuple-element.9.refs_5_), channel_id=1, source_target_pairs={{4,8},{12,16},{20,24},{28,32},{36,40},{44,48},{52,56},{60,64},{68,... | collective-permute-start | bytes 221192 | tf_op jit(solution)/shard_map/ppermute | solution.py:235
  43.2 1.1 %collective-permute-start.1 = (bf16[144,256]{1,0:T(8,128)(2,1)S(1)}, bf16[144,256]{1,0:T(8,128)(2,1)S(1)}, u32[]{:S(2)}, u32[]{:S(2)}) collective-permute-start(bf16[144,256]{1,0:T(8,128)(2,1)S(1)} %get-tuple-element.10.refs_6_), channel_id=1, source_target_pairs={{0,4},{8,12},{16,20},{24,28},{32,36},{40,44},{48,52},{56,60},{64,6... | collective-permute-start | bytes 221192 | tf_op jit(solution)/shard_map/ppermute | solution.py:235
  44.3 3.0 %shard_map.56 = (f32[8,144,128]{2,1,0:T(8,128)S(1)}, bf16[8,256,512]{2,1,0:T(8,128)(2,1)S(1)}) custom-call(bf16[64,2,4096]{2,1,0:T(2,128)(2,1)S(1)} %bitcast.8, s32[8,256]{1,0:T(8,128)S(1)} %bitcast.11, s32[1,8]{1,0:T(1,128)S(1)} %copy-done.3, f32[8,256]{1,0:T(8,128)S(1)} %bitcast.13, f32[8,256]{1,0:T(8,128)S(1)} %bitcast.15, ...), custom_call_target="tpu_custom_call" | custom-call | flops 5000000000 | bytes 1220640 | tf_op jit(solution)/shard_map/pallas_call | solution.py:203
  47.3 0.0 collective-permute-done.refs_2_
  47.3 0.0 collective-permute-done.1.refs_3_
  47.3 2.7 %shard_map.57 = bf16[64,2,4096]{2,1,0:T(2,128)(2,1)S(1)} custom-call(f32[8,144,128]{2,1,0:T(8,128)S(1)} %get-tuple-element.11.refs_0_, bf16[8,256,512]{2,1,0:T(8,128)(2,1)S(1)} %get-tuple-element.12.refs_1_, bf16[144,256]{1,0:T(8,128)(2,1)S(1)} %collective-permute-done.refs_2_, bf16[144,256]{1,0:T(8,128)(2,1)S(1)} %collective-permute-done.1.refs_3_), custom_call_target="tpu_custom_call" | custom-call | flops 5000000000 | bytes 2834432 | tf_op jit(solution)/shard_map/pallas_call | solution.py:203
  50.0 34.4 %all_to_all.19 = bf16[2,64,4096]{2,0,1:T(2,128)(2,1)S(1)} all-to-all(bf16[2,64,4096]{2,0,1:T(2,128)(2,1)S(1)} %bitcast.9), channel_id=1, replica_groups=mesh['mem'=64,'blk'=4] {'mem'}, dimensions={1} | all-to-all | bytes 2097152 | tf_op jit(solution)/shard_map/all_to_all | solution.py:245
  84.4 1.0 %copy.7 = bf16[2,262144]{1,0:T(2,128)(2,1)} copy(bf16[2,262144]{1,0:T(2,128)(2,1)S(1)} %bitcast.16) | data formatting | bytes 2097152
Async XLA Ops:
  0.0 41.7 %copy-start = (s32[1,8,256]{2,1,0:T(8,128)S(1)}, s32[1,8,256]{2,1,0:T(8,128)}, u32[]{:S(2)}) copy-start(s32[1,8,256]{2,1,0:T(8,128)} %param.6) | copy-start | bytes 24580
  0.0 41.7 %copy-start.1 = (f32[1,8,256]{2,1,0:T(8,128)S(1)}, f32[1,8,256]{2,1,0:T(8,128)}, u32[]{:S(2)}) copy-start(f32[1,8,256]{2,1,0:T(8,128)} %param.8) | copy-start | bytes 24580
  0.0 41.7 %copy-start.2 = (f32[1,8,256]{2,1,0:T(8,128)S(1)}, f32[1,8,256]{2,1,0:T(8,128)}, u32[]{:S(2)}) copy-start(f32[1,8,256]{2,1,0:T(8,128)} %param.9) | copy-start | bytes 24580
  0.0 41.7 %copy-start.3 = (s32[1,8]{1,0:T(1,128)S(1)}, s32[1,8]{1,0:T(1,128)}, u32[]{:S(2)}) copy-start(s32[1,8]{1,0:T(1,128)} %refs_2_.3) | copy-start | bytes 100
  42.1 5.2 %collective-permute-start = (bf16[144,256]{1,0:T(8,128)(2,1)S(1)}, bf16[144,256]{1,0:T(8,128)(2,1)S(1)}, u32[]{:S(2)}, u32[]{:S(2)}) collective-permute-start(bf16[144,256]{1,0:T(8,128)(2,1)S(1)} %get-tuple-element.9.refs_5_), channel_id=1, source_target_pairs={{4,8},{12,16},{20,24},{28,32},{36,40},{44,48},{52,56},{60,64},{68,... | collective-permute-start | bytes 221192 | tf_op jit(solution)/shard_map/ppermute | solution.py:235
  43.2 4.1 %collective-permute-start.1 = (bf16[144,256]{1,0:T(8,128)(2,1)S(1)}, bf16[144,256]{1,0:T(8,128)(2,1)S(1)}, u32[]{:S(2)}, u32[]{:S(2)}) collective-permute-start(bf16[144,256]{1,0:T(8,128)(2,1)S(1)} %get-tuple-element.10.refs_6_), channel_id=1, source_target_pairs={{0,4},{8,12},{16,20},{24,28},{32,36},{40,44},{48,52},{56,60},{64,6... | collective-permute-start | bytes 221192 | tf_op jit(solution)/shard_map/ppermute | solution.py:235

commit v4 on v3

--- a/solution.py
+++ b/solution.py
@@ -51,8 +51,11 @@
     return values, jnp.sum(values, axis=0, keepdims=True) * (1.0 / members.shape[0])
 
 
-def rows_of(members, average, cells, count, obs_value, obs_rinv):
-    width, slots = members.shape[1], cells.shape[1]
+def rows_of(b, blocks, members, average, obs_ref):
+    width, slots = members.shape[1], obs_ref.shape[1]
+    cells = obs_ref[b : b + 1].astype(jnp.int32)
+    obs_value = obs_ref[blocks + b : blocks + b + 1]
+    root = obs_ref[2 * blocks + b : 2 * blocks + b + 1]
     high = average.astype(BF).astype(F32)
     rest = average - high
     middle = rest.astype(BF).astype(F32)
@@ -65,8 +68,6 @@
     sampled = dot(stacked, selector)
     size = members.shape[0]
     mean_at = jnp.sum(sampled[size:], axis=0, keepdims=True)
-    slot = lax.broadcasted_iota(jnp.int32, (1, slots), 1)
-    root = jnp.where(slot < count, jnp.sqrt(obs_rinv), 0.0)
     upper = (sampled[:size] - mean_at) * root
     lower = root * (obs_value - mean_at)
     line = lax.broadcasted_iota(jnp.int32, (ROWS - size, slots), 0)
@@ -121,23 +122,17 @@
     return (increment + dot(low, deviation[:128])).astype(BF)
 
 
-def block_rows(b, members, average, obs_refs):
-    cell_ref, count_ref, value_ref, rinv_ref = obs_refs
-    one = slice(b, b + 1)
-    return rows_of(members, average, cell_ref[one], count_ref[0:1, one], value_ref[one], rinv_ref[one])
-
-
 def is_even():
     return lax.rem(lax.axis_index("mem"), 2) == 0
 
 
-def boundary_kernel(blocks, x_ref, cell_ref, count_ref, value_ref, rinv_ref, across_ref, partner_ref):
+def boundary_kernel(blocks, x_ref, obs_ref, across_ref, partner_ref):
     width = x_ref.shape[2] // blocks
     rows = []
     for b in (0, blocks - 1):
         members = members_of(x_ref, b, width)
         _, average = centre(members)
-        rows.append(block_rows(b, members, average, (cell_ref, count_ref, value_ref, rinv_ref)))
+        rows.append(rows_of(b, blocks, members, average, obs_ref))
     first, last = rows
 
     @pl.when(is_even())
@@ -157,9 +152,7 @@
     return jnp.where(even, across, partner), jnp.where(even, partner, across)
 
 
-def gram_kernel(
-    blocks, x_ref, cell_ref, count_ref, value_ref, rinv_ref, across_ref, partner_ref, local_ref, dev_ref
-):
+def gram_kernel(blocks, x_ref, obs_ref, across_ref, partner_ref, local_ref, dev_ref):
     width = x_ref.shape[2] // blocks
     first_gram, last_gram = ordered(across_ref, partner_ref)
     grams = []
@@ -174,7 +167,7 @@
         elif b == blocks - 1:
             grams.append(last_gram)
         else:
-            grams.append(gram_of(block_rows(b, members, average, (cell_ref, count_ref, value_ref, rinv_ref))))
+            grams.append(gram_of(rows_of(b, blocks, members, average, obs_ref)))
         if b > 0:
             below = grams[b - 1]
             if b > 1:
@@ -210,39 +203,59 @@
     )(*args)
 
 
-def analyse(arrived, cells, counts, obs_value, obs_rinv, exchange):
-    blocks, slots = cells.shape
+def packed(obs_cell, obs_count, obs_value, obs_rinv):
+    slot = lax.broadcasted_iota(jnp.int32, obs_cell.shape, 1)
+    root = jnp.where(slot < obs_count[:, None], jnp.sqrt(obs_rinv), 0.0)
+    return jnp.concatenate([obs_cell.astype(F32), obs_value, root], axis=0)
+
+
+def analyse(arrived, obs, exchange):
+    blocks, slots = obs.shape[0] // 3, obs.shape[1]
     kernel = lambda body: (lambda *refs: body(blocks, *refs))
     rows = jax.ShapeDtypeStruct((ROWS, slots), BF)
-    obs = (cells, counts, obs_value, obs_rinv)
-    across, partner = call(kernel(boundary_kernel), (rows, rows), (arrived,) + obs, 2 * 10**8)
+    across, partner = call(kernel(boundary_kernel), (rows, rows), (arrived, obs), 2 * 10**8)
     halo = exchange(across, partner)
     localized = jax.ShapeDtypeStruct((blocks, ROWS, 128), F32)
     deviation = jax.ShapeDtypeStruct((blocks, 256, arrived.shape[2] // blocks), BF)
     localized, deviation = call(
-        kernel(gram_kernel), (localized, deviation), (arrived,) + obs + (across, partner), 5 * 10**9
+        kernel(gram_kernel), (localized, deviation), (arrived, obs, across, partner), 5 * 10**9
     )
     return call(
         kernel(analysis_kernel), jax.ShapeDtypeStruct(arrived.shape, BF), (localized, deviation) + halo, 5 * 10**9
     )
 
 
-def swap_boundaries(across, partner):
-    count = lax.axis_size("mem")
-    hops = [(i, (i + 1) % count) for i in range(1, count, 2)]
-    cores = [(i, i + 1) for i in range(0, count, 2)]
-    both_ways = lambda pairs: pairs + [(target, source) for source, target in pairs]
-    return lax.ppermute(across, "mem", both_ways(hops)), lax.ppermute(partner, "mem", both_ways(cores))
+def snake():
+    columns, deep, cores = 4, 8, 2
+    order = []
+    for x in range(columns):
+        for z in range(deep) if x % 2 == 0 else reversed(range(deep)):
+            order += [(x * deep + z) * cores + core for core in range(cores)]
+    return order
 
 
 def on_device(ensemble, obs_cell, obs_count, obs_value, obs_rinv):
+    order = snake()
     groups = lax.axis_size("mem")
+    assert len(order) == groups
     local, cells = ensemble.shape
-    arrived = lax.all_to_all(ensemble, "mem", split_axis=1, concat_axis=1, tiled=True)
-    arrived = arrived.reshape(local, groups, cells // groups).transpose(1, 0, 2)
-    outgoing = analyse(arrived, obs_cell[0], obs_count, obs_value[0], obs_rinv[0], swap_boundaries)
-    outgoing = outgoing.transpose(1, 0, 2).reshape(local, cells)
-    return lax.all_to_all(outgoing, "mem", split_axis=1, concat_axis=1, tiled=True)
+
+    def swapped(array, pairs):
+        return lax.ppermute(array, "mem", pairs + [(target, source) for source, target in pairs])
+
+    def swap_boundaries(across, partner):
+        hops = [(order[i], order[(i + 1) % groups]) for i in range(1, groups, 2)]
+        cores = [(order[i], order[i + 1]) for i in range(0, groups, 2)]
+        return swapped(across, hops), swapped(partner, cores)
+
+    def exchanged(array):
+        return lax.all_to_all(array, "mem", split_axis=1, concat_axis=1, tiled=True, axis_index_groups=[order])
+
+    arrived = exchanged(ensemble).reshape(local, groups, cells // groups).transpose(1, 0, 2)
+    obs = packed(obs_cell[0], obs_count[0], obs_value[0], obs_rinv[0])
+    obs = lax.ppermute(obs, "mem", list(enumerate(order)))
+    outgoing = analyse(arrived, obs, swap_boundaries)
+    return exchanged(outgoing.transpose(1, 0, 2).reshape(local, cells))
 
 
 def solution(mesh):

time: 85.6 us -> 86.8 us (1.014)
  blocking collectives: 76.1 us -> 35.3 us
  waiting for transfers between devices: 0.01 us -> 27.8 us
  starting transfers between devices: 2.12 us -> 16.2 us
    all_to_all x2 -> x1, blocking collectives: 76.1 us -> 35.3 us  [exchanged(): lax.all_to_all(array, 'mem', split_axis=1, concat_axis=1, tiled=True, axi...]
    all_to_all x0 -> x1, waiting for transfers between devices: none -> 27.8 us  [exchanged(): lax.all_to_all(array, 'mem', split_axis=1, concat_axis=1, tiled=True, axi...]
    all_to_all x0 -> x1, starting transfers between devices: none -> 13.1 us  [exchanged(): lax.all_to_all(array, 'mem', split_axis=1, concat_axis=1, tiled=True, axi...]
    ppermute x2 -> x3, starting transfers between devices: 2.12 us -> 3.08 us  [the longest x2 2.42 us: swapped(): lax.ppermute(array, 'mem', pairs + [(target, source) for source, target i...]
  transfers between devices with their start and end apart: 2 -> 4, of which waited for: 0 -> 1; matrix products, arithmetic and copies ran while one was open for 0% -> 0% of each run, Pallas kernels for 4% -> 4%
where the time goes in v4:
time: 86.8 us; the launch traced here: 86.5 us
  blocking collectives  35.3 us (41%)
  waiting for transfers between devices  27.8 us (32%)
  starting transfers between devices  16.2 us (19%)
  Pallas kernels  6.11 us (7%)
  local copies, waits for them, and re-layouts  0.99 us (1%)
    all_to_all x1, blocking collectives, exchanged(): lax.all_to_all(array, 'mem', split_axis=1, concat_axis=1, tiled=True, axi...  35.3 us
    all_to_all x1, waiting for transfers between devices, exchanged(): lax.all_to_all(array, 'mem', split_axis=1, concat_axis=1, tiled=True, axi...  27.8 us
    all_to_all x1, starting transfers between devices, exchanged(): lax.all_to_all(array, 'mem', split_axis=1, concat_axis=1, tiled=True, axi...  13.1 us
    pallas_call x3, Pallas kernels, call(): pl.pallas_call(kernel, out_shape=out_shape, in_specs=[VMEM] * len(args),...  6.11 us
    ppermute x2, starting transfers between devices, swapped(): lax.ppermute(array, 'mem', pairs + [(target, source) for source, target i...  2.42 us
  transfers between devices with their start and end apart: 4, of which 1 were waited for; matrix products, arithmetic and copies ran while one was open for 0% of the time, Pallas kernels for 4%

profile of v4, /device:TPU:1, one launch (start us, length us, event | category | flops | bytes accessed | tf_op | source)
XLA Modules:
  0.0 86.5 jit_solution(7980394002666691960)
XLA Ops:
  0.0 0.0 copy-start
  0.0 0.0 copy-start.3
  0.0 0.0 copy-start.1
  0.0 0.0 copy-start.2
  0.0 13.1 %all-to-all-start = ((bf16[2,64,4096]{2,0,1:T(2,128)(2,1)}), bf16[2,64,4096]{2,0,1:T(2,128)(2,1)S(1)}, u32[]{:S(2)}, u32[]{:S(2)}) async-start(bf16[2,64,4096]{2,0,1:T(2,128)(2,1)} %bitcast.14), calls=%async_computation | async-start | bytes 2097152 | tf_op jit(solution)/shard_map/all_to_all | solution.py:252
  13.2 0.0 copy-done
  13.2 0.0 copy-done.3
  13.2 0.0 copy-done.1
  13.2 0.1 bitcast_select_fusion
  13.3 0.0 copy-done.2
  13.3 0.7 collective-permute-start
  13.9 0.0 collective-permute-done.refs_1_
  13.9 27.8 %all-to-all-done = bf16[2,64,4096]{2,0,1:T(2,128)(2,1)S(1)} async-done(((bf16[2,64,4096]{2,0,1:T(2,128)(2,1)}), bf16[2,64,4096]{2,0,1:T(2,128)(2,1)S(1)}, u32[]{:S(2)}, u32[]{:S(2)}) %all-to-all-start) | async-done | bytes 1048608 | tf_op jit(solution)/shard_map/all_to_all | solution.py:252
  41.7 0.4 shard_map.55
  42.1 2.4 %collective-permute-start.1 = (bf16[144,256]{1,0:T(8,128)(2,1)S(1)}, bf16[144,256]{1,0:T(8,128)(2,1)S(1)}, u32[]{:S(2)}, u32[]{:S(2)}) collective-permute-start(bf16[144,256]{1,0:T(8,128)(2,1)S(1)} %get-tuple-element.9.refs_2_), channel_id=1, source_target_pairs={{4,8},{12,16},{20,24},{28,32},{36,40},{44,48},{52,56},{60,120},{12... | collective-permute-start | bytes 221192 | tf_op jit(solution)/shard_map/ppermute | solution.py:244
  44.5 0.0 collective-permute-start.2
  44.5 3.0 %shard_map.56 = (f32[8,144,128]{2,1,0:T(8,128)S(1)}, bf16[8,256,512]{2,1,0:T(8,128)(2,1)S(1)}) custom-call(bf16[64,2,4096]{2,1,0:T(2,128)(2,1)S(1)} %bitcast.11, f32[24,256]{1,0:T(8,128)S(1)} %collective-permute-done.refs_1_, bf16[144,256]{1,0:T(8,128)(2,1)S(1)} %get-tuple-element.9.refs_2_, bf16[144,256]{1,0:T(8,128)(2,1)S(1)} %get-tuple-element.10.refs_3_), custom_call_target="tpu_custom_call" | custom-call | flops 5000000000 | bytes 1220608 | tf_op jit(solution)/shard_map/pallas_call | solution.py:196
  47.6 0.0 collective-permute-done.1.refs_2_
  47.6 0.0 collective-permute-done.2.refs_3_
  47.6 2.7 %shard_map.57 = bf16[64,2,4096]{2,1,0:T(2,128)(2,1)S(1)} custom-call(f32[8,144,128]{2,1,0:T(8,128)S(1)} %get-tuple-element.11.refs_0_, bf16[8,256,512]{2,1,0:T(8,128)(2,1)S(1)} %get-tuple-element.12.refs_1_, bf16[144,256]{1,0:T(8,128)(2,1)S(1)} %collective-permute-done.1.refs_2_, bf16[144,256]{1,0:T(8,128)(2,1)S(1)} %collective-permute-done.2.refs_3_), custom_call_target="tpu_custom_call" | custom-call | flops 5000000000 | bytes 2834432 | tf_op jit(solution)/shard_map/pallas_call | solution.py:196
  50.3 35.3 %all_to_all.18 = bf16[2,64,4096]{2,0,1:T(2,128)(2,1)S(1)} all-to-all(bf16[2,64,4096]{2,0,1:T(2,128)(2,1)S(1)} %bitcast.12), channel_id=1, replica_groups={{0,4,8,12,16,20,24,28,32,36,40,44,48,52,56,60,120,124,112,116,104,108,9..., dimensions={1} | all-to-all | bytes 2097152 | tf_op jit(solution)/shard_map/all_to_all | solution.py:252
  85.6 1.0 %copy.7 = bf16[2,262144]{1,0:T(2,128)(2,1)} copy(bf16[2,262144]{1,0:T(2,128)(2,1)S(1)} %bitcast.13) | data formatting | bytes 2097152
  (2 shorter events, 0.0 us)
Async XLA Ops:
  0.0 13.2 %copy-start = (s32[1,8,256]{2,1,0:T(8,128)S(1)}, s32[1,8,256]{2,1,0:T(8,128)}, u32[]{:S(2)}) copy-start(s32[1,8,256]{2,1,0:T(8,128)} %param.6) | copy-start | bytes 24580
  0.0 13.2 %copy-start.3 = (s32[1,8]{1,0:T(1,128)S(1)}, s32[1,8]{1,0:T(1,128)}, u32[]{:S(2)}) copy-start(s32[1,8]{1,0:T(1,128)} %param.7) | copy-start | bytes 100
  0.0 13.2 %copy-start.1 = (f32[1,8,256]{2,1,0:T(8,128)S(1)}, f32[1,8,256]{2,1,0:T(8,128)}, u32[]{:S(2)}) copy-start(f32[1,8,256]{2,1,0:T(8,128)} %param.9) | copy-start | bytes 24580
  0.0 13.3 %copy-start.2 = (f32[1,8,256]{2,1,0:T(8,128)S(1)}, f32[1,8,256]{2,1,0:T(8,128)}, u32[]{:S(2)}) copy-start(f32[1,8,256]{2,1,0:T(8,128)} %param.8) | copy-start | bytes 24580
  0.0 41.7 %all-to-all-start = ((bf16[2,64,4096]{2,0,1:T(2,128)(2,1)}), bf16[2,64,4096]{2,0,1:T(2,128)(2,1)S(1)}, u32[]{:S(2)}, u32[]{:S(2)}) async-start(bf16[2,64,4096]{2,0,1:T(2,128)(2,1)} %bitcast.14), calls=%async_computation | async-start | bytes 2097152 | tf_op jit(solution)/shard_map/all_to_all | solution.py:252
  13.3 0.7 collective-permute-start
  42.1 5.5 %collective-permute-start.1 = (bf16[144,256]{1,0:T(8,128)(2,1)S(1)}, bf16[144,256]{1,0:T(8,128)(2,1)S(1)}, u32[]{:S(2)}, u32[]{:S(2)}) collective-permute-start(bf16[144,256]{1,0:T(8,128)(2,1)S(1)} %get-tuple-element.9.refs_2_), channel_id=1, source_target_pairs={{4,8},{12,16},{20,24},{28,32},{36,40},{44,48},{52,56},{60,120},{12... | collective-permute-start | bytes 221192 | tf_op jit(solution)/shard_map/ppermute | solution.py:244
  44.5 3.1 %collective-permute-start.2 = (bf16[144,256]{1,0:T(8,128)(2,1)S(1)}, bf16[144,256]{1,0:T(8,128)(2,1)S(1)}, u32[]{:S(2)}, u32[]{:S(2)}) collective-permute-start(bf16[144,256]{1,0:T(8,128)(2,1)S(1)} %get-tuple-element.10.refs_3_), channel_id=1, source_target_pairs={{0,4},{8,12},{16,20},{24,28},{32,36},{40,44},{48,52},{56,60},{120,... | collective-permute-start | bytes 221192 | tf_op jit(solution)/shard_map/ppermute | solution.py:244

commit v5 on v3

--- a/solution.py
+++ b/solution.py
@@ -46,32 +46,28 @@
     return piece.reshape(piece.shape[0] * piece.shape[1], width)
 
 
-def centre(members):
-    values = members.astype(F32)
-    return values, jnp.sum(values, axis=0, keepdims=True) * (1.0 / members.shape[0])
-
-
-def rows_of(members, average, cells, count, obs_value, obs_rinv):
-    width, slots = members.shape[1], cells.shape[1]
-    high = average.astype(BF).astype(F32)
-    rest = average - high
-    middle = rest.astype(BF).astype(F32)
-    low = rest - middle
-    line = lax.broadcasted_iota(jnp.int32, (16, width), 0)
-    pieces = jnp.where(line == 0, high, jnp.where(line == 1, middle, jnp.where(line == 2, low, 0.0)))
-    stacked = jnp.concatenate([members, pieces.astype(BF)], axis=0)
-    position = lax.broadcasted_iota(jnp.int32, (width, slots), 0)
-    selector = jnp.where(position == cells, 1.0, 0.0).astype(BF)
-    sampled = dot(stacked, selector)
-    size = members.shape[0]
-    mean_at = jnp.sum(sampled[size:], axis=0, keepdims=True)
+def sample(members, cells):
+    position = lax.broadcasted_iota(jnp.int32, (members.shape[1], cells.shape[1]), 0)
+    return dot(members, jnp.where(position == cells, 1.0, 0.0).astype(BF))
+
+
+def weigh(sampled, count, obs_value, obs_rinv):
+    size, slots = sampled.shape
+    mean_at = jnp.sum(sampled, axis=0, keepdims=True) * (1.0 / size)
     slot = lax.broadcasted_iota(jnp.int32, (1, slots), 1)
     root = jnp.where(slot < count, jnp.sqrt(obs_rinv), 0.0)
-    upper = (sampled[:size] - mean_at) * root
-    lower = root * (obs_value - mean_at)
     line = lax.broadcasted_iota(jnp.int32, (ROWS - size, slots), 0)
-    lower = jnp.where(line == 0, lower, 0.0)
-    return jnp.concatenate([upper, lower], axis=0).astype(BF)
+    lower = jnp.where(line == 0, root * (obs_value - mean_at), 0.0)
+    return jnp.concatenate([((sampled - mean_at) * root).astype(BF), lower.astype(BF)], axis=0)
+
+
+def rows_of(chosen, blocks, x_ref, cell_ref, count_ref, value_ref, rinv_ref):
+    width = x_ref.shape[2] // blocks
+    one = lambda b: slice(b, b + 1)
+    sampled = [sample(members_of(x_ref, b, width), cell_ref[one(b)]) for b in chosen]
+    return [
+        weigh(s, count_ref[0:1, one(b)], value_ref[one(b)], rinv_ref[one(b)]) for b, s in zip(chosen, sampled)
+    ]
 
 
 def gram_of(rows):
@@ -115,16 +111,19 @@
     return out
 
 
-def apply_to(transform, deviation):
-    high, low = split(transform)
-    increment = dot(jnp.concatenate([high, high], axis=1), deviation)
-    return (increment + dot(low, deviation[:128])).astype(BF)
-
-
-def block_rows(b, members, average, obs_refs):
-    cell_ref, count_ref, value_ref, rinv_ref = obs_refs
-    one = slice(b, b + 1)
-    return rows_of(members, average, cell_ref[one], count_ref[0:1, one], value_ref[one], rinv_ref[one])
+def apply_to(transform, members):
+    size = transform.shape[0]
+    pieces, rest = [], transform
+    for _ in range(3):
+        pieces.append(rest.astype(BF))
+        rest = rest - pieces[-1].astype(F32)
+    line = lax.broadcasted_iota(jnp.int32, (16, 3 * size), 0)
+    lane = lax.broadcasted_iota(jnp.int32, (16, 3 * size), 1)
+    ones = jnp.where(jnp.logical_and(line == 0, lane < size), 1.0, 0.0).astype(BF)
+    left = jnp.concatenate([jnp.concatenate(pieces, axis=1), ones], axis=0)
+    product = dot(left, jnp.concatenate([members] * 3, axis=0))
+    average = product[size : size + 1] * (1.0 / size)
+    return (product[:size] - jnp.sum(transform, axis=1, keepdims=True) * average).astype(BF)
 
 
 def is_even():
@@ -132,13 +131,7 @@
 
 
 def boundary_kernel(blocks, x_ref, cell_ref, count_ref, value_ref, rinv_ref, across_ref, partner_ref):
-    width = x_ref.shape[2] // blocks
-    rows = []
-    for b in (0, blocks - 1):
-        members = members_of(x_ref, b, width)
-        _, average = centre(members)
-        rows.append(block_rows(b, members, average, (cell_ref, count_ref, value_ref, rinv_ref)))
-    first, last = rows
+    first, last = rows_of((0, blocks - 1), blocks, x_ref, cell_ref, count_ref, value_ref, rinv_ref)
 
     @pl.when(is_even())
     def _():
@@ -157,41 +150,33 @@
     return jnp.where(even, across, partner), jnp.where(even, partner, across)
 
 
-def gram_kernel(
-    blocks, x_ref, cell_ref, count_ref, value_ref, rinv_ref, across_ref, partner_ref, local_ref, dev_ref
+def finish(chosen, blocks, localized, x_ref, out_ref, offset):
+    width = x_ref.shape[2] // blocks
+    for b, transform in zip(chosen, transforms(localized, eye_of(128))):
+        result = apply_to(transform, members_of(x_ref, b, width))
+        place = slice((b + offset) * width, (b + offset + 1) * width)
+        out_ref[:, :, place] = result.reshape(x_ref.shape[0], x_ref.shape[1], width)
+
+
+def interior_kernel(
+    blocks, x_ref, cell_ref, count_ref, value_ref, rinv_ref, across_ref, partner_ref, inner_ref, part_ref
 ):
+    first, last = ordered(across_ref, partner_ref)
+    chosen = range(1, blocks - 1)
+    rows = rows_of(chosen, blocks, x_ref, cell_ref, count_ref, value_ref, rinv_ref)
+    grams = [first] + [gram_of(r) for r in rows] + [last]
+    part_ref[0] = grams[0] + localize * grams[1]
+    part_ref[1] = grams[-1] + localize * grams[-2]
+    localized = [grams[b] + localize * (grams[b - 1] + grams[b + 1]) for b in chosen]
+    finish(chosen, blocks, localized, x_ref, inner_ref, -1)
+
+
+def analysis_kernel(blocks, x_ref, part_ref, across_ref, partner_ref, inner_ref, out_ref):
     width = x_ref.shape[2] // blocks
-    first_gram, last_gram = ordered(across_ref, partner_ref)
-    grams = []
-    for b in range(blocks):
-        members = members_of(x_ref, b, width)
-        values, average = centre(members)
-        high, low = split(values - average)
-        dev_ref[b, :128] = high
-        dev_ref[b, 128:] = low
-        if b == 0:
-            grams.append(first_gram)
-        elif b == blocks - 1:
-            grams.append(last_gram)
-        else:
-            grams.append(gram_of(block_rows(b, members, average, (cell_ref, count_ref, value_ref, rinv_ref))))
-        if b > 0:
-            below = grams[b - 1]
-            if b > 1:
-                below = below + localize * grams[b - 2]
-            local_ref[b - 1] = below + localize * grams[b]
-    local_ref[blocks - 1] = grams[blocks - 1] + localize * grams[blocks - 2]
-
-
-def analysis_kernel(blocks, local_ref, dev_ref, across_ref, partner_ref, out_ref):
-    width = out_ref.shape[2] // blocks
-    localized = [local_ref[b] for b in range(blocks)]
     left, right = ordered(across_ref, partner_ref)
-    localized[0] = localized[0] + localize * left
-    localized[-1] = localized[-1] + localize * right
-    for b, transform in enumerate(transforms(localized, eye_of(128))):
-        result = apply_to(transform, dev_ref[b])
-        out_ref[:, :, b * width : (b + 1) * width] = result.reshape(out_ref.shape[0], out_ref.shape[1], width)
+    localized = [part_ref[0] + localize * left, part_ref[1] + localize * right]
+    out_ref[:, :, width : (blocks - 1) * width] = inner_ref[...]
+    finish((0, blocks - 1), blocks, localized, x_ref, out_ref, 0)
 
 
 VMEM = pl.BlockSpec(memory_space=pltpu.VMEM)
@@ -217,13 +202,13 @@
     obs = (cells, counts, obs_value, obs_rinv)
     across, partner = call(kernel(boundary_kernel), (rows, rows), (arrived,) + obs, 2 * 10**8)
     halo = exchange(across, partner)
-    localized = jax.ShapeDtypeStruct((blocks, ROWS, 128), F32)
-    deviation = jax.ShapeDtypeStruct((blocks, 256, arrived.shape[2] // blocks), BF)
-    localized, deviation = call(
-        kernel(gram_kernel), (localized, deviation), (arrived,) + obs + (across, partner), 5 * 10**9
+    inner = jax.ShapeDtypeStruct(arrived.shape[:2] + (arrived.shape[2] // blocks * (blocks - 2),), BF)
+    part = jax.ShapeDtypeStruct((2, ROWS, 128), F32)
+    inner, part = call(
+        kernel(interior_kernel), (inner, part), (arrived,) + obs + (across, partner), 5 * 10**9
     )
     return call(
-        kernel(analysis_kernel), jax.ShapeDtypeStruct(arrived.shape, BF), (localized, deviation) + halo, 5 * 10**9
+        kernel(analysis_kernel), jax.ShapeDtypeStruct(arrived.shape, BF), (arrived, part) + halo + (inner,), 2 * 10**9
     )
 
 

time: 85.6 us -> 85.5 us (level)
  no operation moved by 1% of the time
where the time goes in v5:
time: 85.5 us; the launch traced here: 85.2 us
  blocking collectives  75.9 us (89%)
  Pallas kernels  5.58 us (7%)
  starting transfers between devices  2.12 us (2%)
  local copies, waits for them, and re-layouts  1.63 us (2%)
    all_to_all x1, blocking collectives, on_device(): lax.all_to_all(ensemble, 'mem', split_axis=1, concat_axis=1, tiled=True)  41.7 us
    all_to_all x1, blocking collectives, on_device(): lax.all_to_all(outgoing, 'mem', split_axis=1, concat_axis=1, tiled=True)  34.2 us
    pallas_call x3, Pallas kernels, call(): pl.pallas_call(kernel, out_shape=out_shape, in_specs=[VMEM] * len(args),...  5.58 us
  transfers between devices with their start and end apart: 2, of which 0 were waited for; matrix products, arithmetic and copies ran while one was open for 0% of the time, Pallas kernels for 4%

profile of v5, /device:TPU:1, one launch (start us, length us, event | category | flops | bytes accessed | tf_op | source)
XLA Modules:
  0.0 85.2 jit_solution(10614056778899438260)
XLA Ops:
  0.0 0.0 copy-start
  0.0 0.0 copy-start.1
  0.0 0.0 copy-start.2
  0.0 41.7 %all_to_all.18 = bf16[2,64,4096]{2,0,1:T(2,128)(2,1)S(1)} all-to-all(bf16[2,64,4096]{2,0,1:T(2,128)(2,1)} %bitcast.18), channel_id=1, replica_groups=mesh['mem'=64,'blk'=4] {'mem'}, dimensions={1} | all-to-all | bytes 2097152 | tf_op jit(solution)/shard_map/all_to_all | solution.py:226
  41.7 0.0 copy-start.3
  41.7 0.0 copy-done
  41.7 0.0 copy-done.1
  41.7 0.0 copy-done.2
  41.7 0.6 copy-done.3
  42.3 0.3 shard_map.55
  42.7 1.0 %collective-permute-start = (bf16[144,256]{1,0:T(8,128)(2,1)S(1)}, bf16[144,256]{1,0:T(8,128)(2,1)S(1)}, u32[]{:S(2)}, u32[]{:S(2)}) collective-permute-start(bf16[144,256]{1,0:T(8,128)(2,1)S(1)} %get-tuple-element.9.refs_5_), channel_id=1, source_target_pairs={{4,8},{12,16},{20,24},{28,32},{36,40},{44,48},{52,56},{60,64},{68,... | collective-permute-start | bytes 221192 | tf_op jit(solution)/shard_map/ppermute | solution.py:220
  43.7 1.1 %collective-permute-start.1 = (bf16[144,256]{1,0:T(8,128)(2,1)S(1)}, bf16[144,256]{1,0:T(8,128)(2,1)S(1)}, u32[]{:S(2)}, u32[]{:S(2)}) collective-permute-start(bf16[144,256]{1,0:T(8,128)(2,1)S(1)} %get-tuple-element.10.refs_6_), channel_id=1, source_target_pairs={{0,4},{8,12},{16,20},{24,28},{32,36},{40,44},{48,52},{56,60},{64,6... | collective-permute-start | bytes 221192 | tf_op jit(solution)/shard_map/ppermute | solution.py:220
  44.8 3.2 %shard_map.56 = (bf16[64,2,3072]{2,1,0:T(2,128)(2,1)S(1)}, f32[2,144,128]{2,1,0:T(8,128)S(1)}) custom-call(bf16[64,2,4096]{2,1,0:T(2,128)(2,1)S(1)} %bitcast.8, s32[8,256]{1,0:T(8,128)S(1)} %bitcast.12, s32[1,8]{1,0:T(1,128)S(1)} %copy-done.3, f32[8,256]{1,0:T(8,128)S(1)} %bitcast.14, f32[8,256]{1,0:T(8,128)S(1)} %bitcast.16, ...), custom_call_target="tpu_custom_call" | custom-call | flops 5000000000 | bytes 1220640 | tf_op jit(solution)/shard_map/pallas_call | solution.py:188
  48.0 0.0 collective-permute-done.refs_2_
  48.0 0.0 collective-permute-done.1.refs_3_
  48.0 2.0 %shard_map.57 = bf16[64,2,4096]{2,1,0:T(2,128)(2,1)S(1)} custom-call(bf16[64,2,4096]{2,1,0:T(2,128)(2,1)S(1)} %bitcast.9, f32[2,144,128]{2,1,0:T(8,128)S(1)} %get-tuple-element.11.refs_1_, bf16[144,256]{1,0:T(8,128)(2,1)S(1)} %collective-permute-done.refs_2_, bf16[144,256]{1,0:T(8,128)(2,1)S(1)} %collective-permute-done.1.refs_3_, ...), custom_call_target="tpu_custom_call" | custom-call | flops 2000000000 | bytes 2129920 | tf_op jit(solution)/shard_map/pallas_call | solution.py:188
  50.1 34.2 %all_to_all.19 = bf16[2,64,4096]{2,0,1:T(2,128)(2,1)S(1)} all-to-all(bf16[2,64,4096]{2,0,1:T(2,128)(2,1)S(1)} %bitcast.10), channel_id=1, replica_groups=mesh['mem'=64,'blk'=4] {'mem'}, dimensions={1} | all-to-all | bytes 2097152 | tf_op jit(solution)/shard_map/all_to_all | solution.py:230
  84.3 1.0 %copy.7 = bf16[2,262144]{1,0:T(2,128)(2,1)} copy(bf16[2,262144]{1,0:T(2,128)(2,1)S(1)} %bitcast.17) | data formatting | bytes 2097152
Async XLA Ops:
  0.0 41.7 %copy-start = (s32[1,8,256]{2,1,0:T(8,128)S(1)}, s32[1,8,256]{2,1,0:T(8,128)}, u32[]{:S(2)}) copy-start(s32[1,8,256]{2,1,0:T(8,128)} %param.6) | copy-start | bytes 24580
  0.0 41.7 %copy-start.1 = (f32[1,8,256]{2,1,0:T(8,128)S(1)}, f32[1,8,256]{2,1,0:T(8,128)}, u32[]{:S(2)}) copy-start(f32[1,8,256]{2,1,0:T(8,128)} %param.8) | copy-start | bytes 24580
  0.0 41.7 %copy-start.2 = (f32[1,8,256]{2,1,0:T(8,128)S(1)}, f32[1,8,256]{2,1,0:T(8,128)}, u32[]{:S(2)}) copy-start(f32[1,8,256]{2,1,0:T(8,128)} %param.9) | copy-start | bytes 24580
  41.7 0.7 copy-start.3
  42.7 5.4 %collective-permute-start = (bf16[144,256]{1,0:T(8,128)(2,1)S(1)}, bf16[144,256]{1,0:T(8,128)(2,1)S(1)}, u32[]{:S(2)}, u32[]{:S(2)}) collective-permute-start(bf16[144,256]{1,0:T(8,128)(2,1)S(1)} %get-tuple-element.9.refs_5_), channel_id=1, source_target_pairs={{4,8},{12,16},{20,24},{28,32},{36,40},{44,48},{52,56},{60,64},{68,... | collective-permute-start | bytes 221192 | tf_op jit(solution)/shard_map/ppermute | solution.py:220
  43.7 4.3 %collective-permute-start.1 = (bf16[144,256]{1,0:T(8,128)(2,1)S(1)}, bf16[144,256]{1,0:T(8,128)(2,1)S(1)}, u32[]{:S(2)}, u32[]{:S(2)}) collective-permute-start(bf16[144,256]{1,0:T(8,128)(2,1)S(1)} %get-tuple-element.10.refs_6_), channel_id=1, source_target_pairs={{0,4},{8,12},{16,20},{24,28},{32,36},{40,44},{48,52},{56,60},{64,6... | collective-permute-start | bytes 221192 | tf_op jit(solution)/shard_map/ppermute | solution.py:220

commit v6 on v5

--- a/solution.py
+++ b/solution.py
@@ -51,23 +51,19 @@
     return dot(members, jnp.where(position == cells, 1.0, 0.0).astype(BF))
 
 
-def weigh(sampled, count, obs_value, obs_rinv):
+def weigh(sampled, obs_value, root):
     size, slots = sampled.shape
     mean_at = jnp.sum(sampled, axis=0, keepdims=True) * (1.0 / size)
-    slot = lax.broadcasted_iota(jnp.int32, (1, slots), 1)
-    root = jnp.where(slot < count, jnp.sqrt(obs_rinv), 0.0)
     line = lax.broadcasted_iota(jnp.int32, (ROWS - size, slots), 0)
     lower = jnp.where(line == 0, root * (obs_value - mean_at), 0.0)
     return jnp.concatenate([((sampled - mean_at) * root).astype(BF), lower.astype(BF)], axis=0)
 
 
-def rows_of(chosen, blocks, x_ref, cell_ref, count_ref, value_ref, rinv_ref):
+def rows_of(chosen, blocks, x_ref, obs_ref):
     width = x_ref.shape[2] // blocks
-    one = lambda b: slice(b, b + 1)
-    sampled = [sample(members_of(x_ref, b, width), cell_ref[one(b)]) for b in chosen]
-    return [
-        weigh(s, count_ref[0:1, one(b)], value_ref[one(b)], rinv_ref[one(b)]) for b, s in zip(chosen, sampled)
-    ]
+    of_kind = lambda kind, b: obs_ref[kind * blocks + b : kind * blocks + b + 1]
+    sampled = [sample(members_of(x_ref, b, width), of_kind(0, b).astype(jnp.int32)) for b in chosen]
+    return [weigh(s, of_kind(1, b), of_kind(2, b)) for b, s in zip(chosen, sampled)]
 
 
 def gram_of(rows):
@@ -130,8 +126,8 @@
     return lax.rem(lax.axis_index("mem"), 2) == 0
 
 
-def boundary_kernel(blocks, x_ref, cell_ref, count_ref, value_ref, rinv_ref, across_ref, partner_ref):
-    first, last = rows_of((0, blocks - 1), blocks, x_ref, cell_ref, count_ref, value_ref, rinv_ref)
+def boundary_kernel(blocks, x_ref, obs_ref, across_ref, partner_ref):
+    first, last = rows_of((0, blocks - 1), blocks, x_ref, obs_ref)
 
     @pl.when(is_even())
     def _():
@@ -159,11 +155,11 @@
 
 
 def interior_kernel(
-    blocks, x_ref, cell_ref, count_ref, value_ref, rinv_ref, across_ref, partner_ref, inner_ref, part_ref
+    blocks, x_ref, obs_ref, across_ref, partner_ref, inner_ref, part_ref
 ):
     first, last = ordered(across_ref, partner_ref)
     chosen = range(1, blocks - 1)
-    rows = rows_of(chosen, blocks, x_ref, cell_ref, count_ref, value_ref, rinv_ref)
+    rows = rows_of(chosen, blocks, x_ref, obs_ref)
     grams = [first] + [gram_of(r) for r in rows] + [last]
     part_ref[0] = grams[0] + localize * grams[1]
     part_ref[1] = grams[-1] + localize * grams[-2]
@@ -195,17 +191,22 @@
     )(*args)
 
 
-def analyse(arrived, cells, counts, obs_value, obs_rinv, exchange):
-    blocks, slots = cells.shape
+def packed(obs_cell, obs_count, obs_value, obs_rinv):
+    slot = lax.broadcasted_iota(jnp.int32, obs_cell.shape, 1)
+    root = jnp.where(slot < obs_count[:, None], jnp.sqrt(obs_rinv), 0.0)
+    return jnp.concatenate([obs_cell.astype(F32), obs_value, root], axis=0)
+
+
+def analyse(arrived, obs, exchange):
+    blocks, slots = obs.shape[0] // 3, obs.shape[1]
     kernel = lambda body: (lambda *refs: body(blocks, *refs))
     rows = jax.ShapeDtypeStruct((ROWS, slots), BF)
-    obs = (cells, counts, obs_value, obs_rinv)
-    across, partner = call(kernel(boundary_kernel), (rows, rows), (arrived,) + obs, 2 * 10**8)
+    across, partner = call(kernel(boundary_kernel), (rows, rows), (arrived, obs), 2 * 10**8)
     halo = exchange(across, partner)
     inner = jax.ShapeDtypeStruct(arrived.shape[:2] + (arrived.shape[2] // blocks * (blocks - 2),), BF)
     part = jax.ShapeDtypeStruct((2, ROWS, 128), F32)
     inner, part = call(
-        kernel(interior_kernel), (inner, part), (arrived,) + obs + (across, partner), 5 * 10**9
+        kernel(interior_kernel), (inner, part), (arrived, obs, across, partner), 5 * 10**9
     )
     return call(
         kernel(analysis_kernel), jax.ShapeDtypeStruct(arrived.shape, BF), (arrived, part) + halo + (inner,), 2 * 10**9
@@ -225,7 +226,8 @@
     local, cells = ensemble.shape
     arrived = lax.all_to_all(ensemble, "mem", split_axis=1, concat_axis=1, tiled=True)
     arrived = arrived.reshape(local, groups, cells // groups).transpose(1, 0, 2)
-    outgoing = analyse(arrived, obs_cell[0], obs_count, obs_value[0], obs_rinv[0], swap_boundaries)
+    obs = packed(obs_cell[0], obs_count[0], obs_value[0], obs_rinv[0])
+    outgoing = analyse(arrived, obs, swap_boundaries)
     outgoing = outgoing.transpose(1, 0, 2).reshape(local, cells)
     return lax.all_to_all(outgoing, "mem", split_axis=1, concat_axis=1, tiled=True)
 

time: 85.5 us -> 85 us (level)
  blocking collectives: 75.9 us -> 34.2 us
  waiting for transfers between devices: 0.01 us -> 27.1 us
  starting transfers between devices: 2.12 us -> 15.2 us
    all_to_all x1 -> x0, blocking collectives: 41.7 us -> none  [on_device(): lax.all_to_all(ensemble, 'mem', split_axis=1, concat_axis=1, tiled=True)]
    all_to_all x0 -> x1, waiting for transfers between devices: none -> 27.1 us  [on_device(): lax.all_to_all(ensemble, 'mem', split_axis=1, concat_axis=1, tiled=True)]
    all_to_all x0 -> x1, starting transfers between devices: none -> 13.1 us  [on_device(): lax.all_to_all(ensemble, 'mem', split_axis=1, concat_axis=1, tiled=True)]
  transfers between devices with their start and end apart: 2 -> 3, of which waited for: 0 -> 1; matrix products, arithmetic and copies ran while one was open for 0% -> 0% of each run, Pallas kernels for 4% -> 4%
where the time goes in v6:
time: 85 us; the launch traced here: 84.6 us
  blocking collectives  34.2 us (40%)
  waiting for transfers between devices  27.1 us (32%)
  starting transfers between devices  15.2 us (18%)
  Pallas kernels  5.56 us (7%)
  local copies, waits for them, and re-layouts  2.28 us (3%)
    all_to_all x1, blocking collectives, on_device(): lax.all_to_all(outgoing, 'mem', split_axis=1, concat_axis=1, tiled=True)  34.2 us
    all_to_all x1, waiting for transfers between devices, on_device(): lax.all_to_all(ensemble, 'mem', split_axis=1, concat_axis=1, tiled=True)  27.1 us
    all_to_all x1, starting transfers between devices, on_device(): lax.all_to_all(ensemble, 'mem', split_axis=1, concat_axis=1, tiled=True)  13.1 us
    pallas_call x3, Pallas kernels, call(): pl.pallas_call(kernel, out_shape=out_shape, in_specs=[VMEM] * len(args),...  5.56 us
    unnamed x9, local copies, waits for them, and re-layouts  2.28 us
  transfers between devices with their start and end apart: 3, of which 1 were waited for; matrix products, arithmetic and copies ran while one was open for 0% of the time, Pallas kernels for 4%

profile of v6, /device:TPU:1, one launch (start us, length us, event | category | flops | bytes accessed | tf_op | source)
XLA Modules:
  0.0 84.6 jit_solution(15083709953253266541)
XLA Ops:
  0.0 0.0 copy-start
  0.0 13.1 %all-to-all-start = ((bf16[2,64,4096]{2,0,1:T(2,128)(2,1)}), bf16[2,64,4096]{2,0,1:T(2,128)(2,1)S(1)}, u32[]{:S(2)}, u32[]{:S(2)}) async-start(bf16[2,64,4096]{2,0,1:T(2,128)(2,1)} %bitcast.15), calls=%async_computation | async-start | bytes 2097152 | tf_op jit(solution)/shard_map/all_to_all | solution.py:227
  13.1 0.0 copy-done
  13.1 0.0 copy-start.1
  13.2 0.0 copy-start.3
  13.2 0.7 copy-done.1
  13.8 0.0 copy-done.3
  13.8 0.0 copy-start.2
  13.8 0.1 bitcast_select_fusion
  13.9 0.6 copy-done.2
  14.5 27.1 %all-to-all-done = bf16[2,64,4096]{2,0,1:T(2,128)(2,1)S(1)} async-done(((bf16[2,64,4096]{2,0,1:T(2,128)(2,1)}), bf16[2,64,4096]{2,0,1:T(2,128)(2,1)S(1)}, u32[]{:S(2)}, u32[]{:S(2)}) %all-to-all-start) | async-done | bytes 1048608 | tf_op jit(solution)/shard_map/all_to_all | solution.py:227
  41.7 0.3 shard_map.55
  42.0 1.0 %collective-permute-start = (bf16[144,256]{1,0:T(8,128)(2,1)S(1)}, bf16[144,256]{1,0:T(8,128)(2,1)S(1)}, u32[]{:S(2)}, u32[]{:S(2)}) collective-permute-start(bf16[144,256]{1,0:T(8,128)(2,1)S(1)} %get-tuple-element.9.refs_2_), channel_id=1, source_target_pairs={{4,8},{12,16},{20,24},{28,32},{36,40},{44,48},{52,56},{60,64},{68,... | collective-permute-start | bytes 221192 | tf_op jit(solution)/shard_map/ppermute | solution.py:221
  43.0 1.1 %collective-permute-start.1 = (bf16[144,256]{1,0:T(8,128)(2,1)S(1)}, bf16[144,256]{1,0:T(8,128)(2,1)S(1)}, u32[]{:S(2)}, u32[]{:S(2)}) collective-permute-start(bf16[144,256]{1,0:T(8,128)(2,1)S(1)} %get-tuple-element.10.refs_3_), channel_id=1, source_target_pairs={{0,4},{8,12},{16,20},{24,28},{32,36},{40,44},{48,52},{56,60},{64,6... | collective-permute-start | bytes 221192 | tf_op jit(solution)/shard_map/ppermute | solution.py:221
  44.1 3.2 %shard_map.56 = (bf16[64,2,3072]{2,1,0:T(2,128)(2,1)S(1)}, f32[2,144,128]{2,1,0:T(8,128)S(1)}) custom-call(bf16[64,2,4096]{2,1,0:T(2,128)(2,1)S(1)} %bitcast.11, f32[24,256]{1,0:T(8,128)S(1)} %pad_maximum_fusion.refs_1_, bf16[144,256]{1,0:T(8,128)(2,1)S(1)} %get-tuple-element.9.refs_2_, bf16[144,256]{1,0:T(8,128)(2,1)S(1)} %get-tuple-element.10.refs_3_), custom_call_target="tpu_custom_call" | custom-call | flops 5000000000 | bytes 1220608 | tf_op jit(solution)/shard_map/pallas_call | solution.py:184
  47.3 0.0 collective-permute-done.refs_2_
  47.4 0.0 collective-permute-done.1.refs_3_
  47.4 2.0 %shard_map.57 = bf16[64,2,4096]{2,1,0:T(2,128)(2,1)S(1)} custom-call(bf16[64,2,4096]{2,1,0:T(2,128)(2,1)S(1)} %bitcast.12, f32[2,144,128]{2,1,0:T(8,128)S(1)} %get-tuple-element.11.refs_1_, bf16[144,256]{1,0:T(8,128)(2,1)S(1)} %collective-permute-done.refs_2_, bf16[144,256]{1,0:T(8,128)(2,1)S(1)} %collective-permute-done.1.refs_3_, ...), custom_call_target="tpu_custom_call" | custom-call | flops 2000000000 | bytes 2129920 | tf_op jit(solution)/shard_map/pallas_call | solution.py:184
  49.4 34.2 %all_to_all.18 = bf16[2,64,4096]{2,0,1:T(2,128)(2,1)S(1)} all-to-all(bf16[2,64,4096]{2,0,1:T(2,128)(2,1)S(1)} %bitcast.13), channel_id=1, replica_groups=mesh['mem'=64,'blk'=4] {'mem'}, dimensions={1} | all-to-all | bytes 2097152 | tf_op jit(solution)/shard_map/all_to_all | solution.py:232
  83.6 1.0 %copy.7 = bf16[2,262144]{1,0:T(2,128)(2,1)} copy(bf16[2,262144]{1,0:T(2,128)(2,1)S(1)} %bitcast.14) | data formatting | bytes 2097152
  (2 shorter events, 0.0 us)
Async XLA Ops:
  0.0 13.1 %copy-start = (s32[1,8,256]{2,1,0:T(8,128)S(1)}, s32[1,8,256]{2,1,0:T(8,128)}, u32[]{:S(2)}) copy-start(s32[1,8,256]{2,1,0:T(8,128)} %param.6) | copy-start | bytes 24580
  0.0 41.7 %all-to-all-start = ((bf16[2,64,4096]{2,0,1:T(2,128)(2,1)}), bf16[2,64,4096]{2,0,1:T(2,128)(2,1)S(1)}, u32[]{:S(2)}, u32[]{:S(2)}) async-start(bf16[2,64,4096]{2,0,1:T(2,128)(2,1)} %bitcast.15), calls=%async_computation | async-start | bytes 2097152 | tf_op jit(solution)/shard_map/all_to_all | solution.py:227
  13.1 0.7 copy-start.1
  13.2 0.7 copy-start.3
  13.8 0.7 copy-start.2
  42.0 5.3 %collective-permute-start = (bf16[144,256]{1,0:T(8,128)(2,1)S(1)}, bf16[144,256]{1,0:T(8,128)(2,1)S(1)}, u32[]{:S(2)}, u32[]{:S(2)}) collective-permute-start(bf16[144,256]{1,0:T(8,128)(2,1)S(1)} %get-tuple-element.9.refs_2_), channel_id=1, source_target_pairs={{4,8},{12,16},{20,24},{28,32},{36,40},{44,48},{52,56},{60,64},{68,... | collective-permute-start | bytes 221192 | tf_op jit(solution)/shard_map/ppermute | solution.py:221
  43.0 4.3 %collective-permute-start.1 = (bf16[144,256]{1,0:T(8,128)(2,1)S(1)}, bf16[144,256]{1,0:T(8,128)(2,1)S(1)}, u32[]{:S(2)}, u32[]{:S(2)}) collective-permute-start(bf16[144,256]{1,0:T(8,128)(2,1)S(1)} %get-tuple-element.10.refs_3_), channel_id=1, source_target_pairs={{0,4},{8,12},{16,20},{24,28},{32,36},{40,44},{48,52},{56,60},{64,6... | collective-permute-start | bytes 221192 | tf_op jit(solution)/shard_map/ppermute | solution.py:221

commit v7 on v6

--- a/solution.py
+++ b/solution.py
@@ -20,25 +20,17 @@
 
 
 def left_of(a):
-    return jnp.concatenate(split(a), axis=1)
+    high, low = split(a)
+    return jnp.concatenate([high, low, high], axis=1)
 
 
 def right_of(a):
-    pair = jnp.concatenate(split(a), axis=1)
-    return jnp.concatenate([pair, pair], axis=0)
-
-
-def fold(wide):
-    half = wide.shape[1] // 2
-    return wide[:, :half] + wide[:, half:]
+    high, low = split(a)
+    return jnp.concatenate([high, high, low], axis=0)
 
 
 def dot(a, b):
     return jnp.dot(a, b, preferred_element_type=F32)
-
-
-def mm(left, right):
-    return fold(dot(left, right))
 
 
 def members_of(x_ref, b, width):
@@ -84,21 +76,20 @@
         jnp.max(jnp.sum(jnp.abs(a), axis=0, keepdims=True), axis=1, keepdims=True) for a in systems
     ]
     scales = [1.0 / b for b in bounds]
-    y = [a * s for a, s in zip(systems, scales)]
-    u = [1.5 * eye - 0.5 * a for a in y]
-    z = u
-    y = [mm(left_of(a), right_of(b)) for a, b in zip(y, u)]
+    squares = [dot(left_of(a), right_of(a)) for a in systems]
+    y = [s * (1.5 * a - (0.5 * s) * q) for a, q, s in zip(systems, squares, scales)]
+    z = [1.5 * eye - (0.5 * s) * a for a, s in zip(systems, scales)]
     for iteration in range(NS_ITERS - 1):
-        u = [1.5 * eye - 0.5 * mm(left_of(a), right_of(b)) for a, b in zip(z, y)]
+        u = [1.5 * eye - 0.5 * dot(left_of(a), right_of(b)) for a, b in zip(z, y)]
         if iteration < NS_ITERS - 2:
             both = [
-                mm(jnp.concatenate([left_of(a), left_of(c)], axis=0), right_of(b))
+                dot(jnp.concatenate([left_of(a), left_of(c)], axis=0), right_of(b))
                 for a, c, b in zip(y, z, u)
             ]
             y = [a[:size] for a in both]
             z = [a[size:] for a in both]
         else:
-            z = [mm(left_of(a), right_of(b)) for a, b in zip(z, u)]
+            z = [dot(left_of(a), right_of(b)) for a, b in zip(z, u)]
     out = []
     for a, f, s in zip(z, forcings, scales):
         inner = jnp.sum(a * f, axis=1, keepdims=True)
@@ -146,16 +137,15 @@
     return jnp.where(even, across, partner), jnp.where(even, partner, across)
 
 
-def finish(chosen, blocks, localized, x_ref, out_ref, offset):
-    width = x_ref.shape[2] // blocks
-    for b, transform in zip(chosen, transforms(localized, eye_of(128))):
-        result = apply_to(transform, members_of(x_ref, b, width))
-        place = slice((b + offset) * width, (b + offset + 1) * width)
-        out_ref[:, :, place] = result.reshape(x_ref.shape[0], x_ref.shape[1], width)
+def finish(places, localized, members, out_ref):
+    for place, transform, load in zip(places, transforms(localized, eye_of(128)), members):
+        result = apply_to(transform, load())
+        width = result.shape[1]
+        out_ref[:, :, place * width : (place + 1) * width] = result.reshape(out_ref.shape[:2] + (width,))
 
 
 def interior_kernel(
-    blocks, x_ref, obs_ref, across_ref, partner_ref, inner_ref, part_ref
+    blocks, x_ref, obs_ref, across_ref, partner_ref, inner_ref, part_ref, edge_ref
 ):
     first, last = ordered(across_ref, partner_ref)
     chosen = range(1, blocks - 1)
@@ -164,15 +154,19 @@
     part_ref[0] = grams[0] + localize * grams[1]
     part_ref[1] = grams[-1] + localize * grams[-2]
     localized = [grams[b] + localize * (grams[b - 1] + grams[b + 1]) for b in chosen]
-    finish(chosen, blocks, localized, x_ref, inner_ref, -1)
-
-
-def analysis_kernel(blocks, x_ref, part_ref, across_ref, partner_ref, inner_ref, out_ref):
     width = x_ref.shape[2] // blocks
+    edge_ref[0] = members_of(x_ref, 0, width)
+    edge_ref[1] = members_of(x_ref, blocks - 1, width)
+    members = [lambda b=b: members_of(x_ref, b, width) for b in chosen]
+    finish([b - 1 for b in chosen], localized, members, inner_ref)
+
+
+def analysis_kernel(blocks, edge_ref, part_ref, across_ref, partner_ref, inner_ref, out_ref):
+    width = edge_ref.shape[2]
     left, right = ordered(across_ref, partner_ref)
     localized = [part_ref[0] + localize * left, part_ref[1] + localize * right]
     out_ref[:, :, width : (blocks - 1) * width] = inner_ref[...]
-    finish((0, blocks - 1), blocks, localized, x_ref, out_ref, 0)
+    finish((0, blocks - 1), localized, [lambda: edge_ref[0], lambda: edge_ref[1]], out_ref)
 
 
 VMEM = pl.BlockSpec(memory_space=pltpu.VMEM)
@@ -205,11 +199,12 @@
     halo = exchange(across, partner)
     inner = jax.ShapeDtypeStruct(arrived.shape[:2] + (arrived.shape[2] // blocks * (blocks - 2),), BF)
     part = jax.ShapeDtypeStruct((2, ROWS, 128), F32)
-    inner, part = call(
-        kernel(interior_kernel), (inner, part), (arrived, obs, across, partner), 5 * 10**9
+    edge = jax.ShapeDtypeStruct((2, 128, arrived.shape[2] // blocks), BF)
+    inner, part, edge = call(
+        kernel(interior_kernel), (inner, part, edge), (arrived, obs, across, partner), 5 * 10**9
     )
     return call(
-        kernel(analysis_kernel), jax.ShapeDtypeStruct(arrived.shape, BF), (arrived, part) + halo + (inner,), 2 * 10**9
+        kernel(analysis_kernel), jax.ShapeDtypeStruct(arrived.shape, BF), (edge, part) + halo + (inner,), 2 * 10**9
     )
 
 

time: 85 us -> 84.8 us (level)
  no operation moved by 1% of the time
where the time goes in v7:
time: 84.8 us; the launch traced here: 84.4 us
  blocking collectives  34.2 us (40%)
  waiting for transfers between devices  27.1 us (32%)
  starting transfers between devices  15.2 us (18%)
  Pallas kernels  5.37 us (6%)
  local copies, waits for them, and re-layouts  2.28 us (3%)
    all_to_all x1, blocking collectives, on_device(): lax.all_to_all(outgoing, 'mem', split_axis=1, concat_axis=1, tiled=True)  34.2 us
    all_to_all x1, waiting for transfers between devices, on_device(): lax.all_to_all(ensemble, 'mem', split_axis=1, concat_axis=1, tiled=True)  27.1 us
    all_to_all x1, starting transfers between devices, on_device(): lax.all_to_all(ensemble, 'mem', split_axis=1, concat_axis=1, tiled=True)  13.1 us
    pallas_call x3, Pallas kernels, call(): pl.pallas_call(kernel, out_shape=out_shape, in_specs=[VMEM] * len(args),...  5.37 us
    unnamed x9, local copies, waits for them, and re-layouts  2.28 us
  transfers between devices with their start and end apart: 3, of which 1 were waited for; matrix products, arithmetic and copies ran while one was open for 0% of the time, Pallas kernels for 4%

profile of v7, /device:TPU:1, one launch (start us, length us, event | category | flops | bytes accessed | tf_op | source)
XLA Modules:
  0.0 84.4 jit_solution(773404283741438454)
XLA Ops:
  0.0 0.0 copy-start
  0.0 13.1 %all-to-all-start = ((bf16[2,64,4096]{2,0,1:T(2,128)(2,1)}), bf16[2,64,4096]{2,0,1:T(2,128)(2,1)S(1)}, u32[]{:S(2)}, u32[]{:S(2)}) async-start(bf16[2,64,4096]{2,0,1:T(2,128)(2,1)} %bitcast.14), calls=%async_computation | async-start | bytes 2097152 | tf_op jit(solution)/shard_map/all_to_all | solution.py:222
  13.1 0.0 copy-done
  13.1 0.0 copy-start.1
  13.2 0.0 copy-start.3
  13.2 0.7 copy-done.1
  13.8 0.0 copy-done.3
  13.8 0.0 copy-start.2
  13.8 0.1 bitcast_select_fusion
  13.9 0.6 copy-done.2
  14.5 27.1 %all-to-all-done = bf16[2,64,4096]{2,0,1:T(2,128)(2,1)S(1)} async-done(((bf16[2,64,4096]{2,0,1:T(2,128)(2,1)}), bf16[2,64,4096]{2,0,1:T(2,128)(2,1)S(1)}, u32[]{:S(2)}, u32[]{:S(2)}) %all-to-all-start) | async-done | bytes 1048608 | tf_op jit(solution)/shard_map/all_to_all | solution.py:222
  41.7 0.3 shard_map.55
  42.0 1.0 %collective-permute-start = (bf16[144,256]{1,0:T(8,128)(2,1)S(1)}, bf16[144,256]{1,0:T(8,128)(2,1)S(1)}, u32[]{:S(2)}, u32[]{:S(2)}) collective-permute-start(bf16[144,256]{1,0:T(8,128)(2,1)S(1)} %get-tuple-element.10.refs_2_), channel_id=1, source_target_pairs={{4,8},{12,16},{20,24},{28,32},{36,40},{44,48},{52,56},{60,64},{68,... | collective-permute-start | bytes 221192 | tf_op jit(solution)/shard_map/ppermute | solution.py:216
  43.0 1.1 %collective-permute-start.1 = (bf16[144,256]{1,0:T(8,128)(2,1)S(1)}, bf16[144,256]{1,0:T(8,128)(2,1)S(1)}, u32[]{:S(2)}, u32[]{:S(2)}) collective-permute-start(bf16[144,256]{1,0:T(8,128)(2,1)S(1)} %get-tuple-element.11.refs_3_), channel_id=1, source_target_pairs={{0,4},{8,12},{16,20},{24,28},{32,36},{40,44},{48,52},{56,60},{64,6... | collective-permute-start | bytes 221192 | tf_op jit(solution)/shard_map/ppermute | solution.py:216
  44.1 3.2 %shard_map.56 = (bf16[64,2,3072]{2,1,0:T(2,128)(2,1)S(1)}, f32[2,144,128]{2,1,0:T(8,128)S(1)}, bf16[2,128,512]{2,1,0:T(8,128)(2,1)S(1)}) custom-call(bf16[64,2,4096]{2,1,0:T(2,128)(2,1)S(1)} %bitcast.11, f32[24,256]{1,0:T(8,128)S(1)} %pad_maximum_fusion.refs_1_, bf16[144,256]{1,0:T(8,128)(2,1)S(1)} %get-tuple-element.10.refs_2_, ...), custom_call_target="tpu_custom_call" | custom-call | flops 5000000000 | bytes 1220608 | tf_op jit(solution)/shard_map/pallas_call | solution.py:178
  47.3 0.0 collective-permute-done.refs_2_
  47.3 0.0 collective-permute-done.1.refs_3_
  47.3 1.9 %shard_map.57 = bf16[64,2,4096]{2,1,0:T(2,128)(2,1)S(1)} custom-call(bf16[2,128,512]{2,1,0:T(8,128)(2,1)S(1)} %get-tuple-element.12.refs_0_, f32[2,144,128]{2,1,0:T(8,128)S(1)} %get-tuple-element.13.refs_1_, bf16[144,256]{1,0:T(8,128)(2,1)S(1)} %collective-permute-done.refs_2_, bf16[144,256]{1,0:T(8,128)(2,1)S(1)} %collective-permute-done.1.refs_3_, ...), custom_call_target="tpu_custom_call" | custom-call | flops 2000000000 | bytes 1343488 | tf_op jit(solution)/shard_map/pallas_call | solution.py:178
  49.2 34.2 %all_to_all.18 = bf16[2,64,4096]{2,0,1:T(2,128)(2,1)S(1)} all-to-all(bf16[2,64,4096]{2,0,1:T(2,128)(2,1)S(1)} %bitcast.12), channel_id=1, replica_groups=mesh['mem'=64,'blk'=4] {'mem'}, dimensions={1} | all-to-all | bytes 2097152 | tf_op jit(solution)/shard_map/all_to_all | solution.py:227
  83.4 1.0 %copy.7 = bf16[2,262144]{1,0:T(2,128)(2,1)} copy(bf16[2,262144]{1,0:T(2,128)(2,1)S(1)} %bitcast.13) | data formatting | bytes 2097152
  (2 shorter events, 0.0 us)
Async XLA Ops:
  0.0 13.1 %copy-start = (s32[1,8,256]{2,1,0:T(8,128)S(1)}, s32[1,8,256]{2,1,0:T(8,128)}, u32[]{:S(2)}) copy-start(s32[1,8,256]{2,1,0:T(8,128)} %param.6) | copy-start | bytes 24580
  0.0 41.7 %all-to-all-start = ((bf16[2,64,4096]{2,0,1:T(2,128)(2,1)}), bf16[2,64,4096]{2,0,1:T(2,128)(2,1)S(1)}, u32[]{:S(2)}, u32[]{:S(2)}) async-start(bf16[2,64,4096]{2,0,1:T(2,128)(2,1)} %bitcast.14), calls=%async_computation | async-start | bytes 2097152 | tf_op jit(solution)/shard_map/all_to_all | solution.py:222
  13.1 0.7 copy-start.1
  13.2 0.7 copy-start.3
  13.8 0.7 copy-start.2
  42.0 5.3 %collective-permute-start = (bf16[144,256]{1,0:T(8,128)(2,1)S(1)}, bf16[144,256]{1,0:T(8,128)(2,1)S(1)}, u32[]{:S(2)}, u32[]{:S(2)}) collective-permute-start(bf16[144,256]{1,0:T(8,128)(2,1)S(1)} %get-tuple-element.10.refs_2_), channel_id=1, source_target_pairs={{4,8},{12,16},{20,24},{28,32},{36,40},{44,48},{52,56},{60,64},{68,... | collective-permute-start | bytes 221192 | tf_op jit(solution)/shard_map/ppermute | solution.py:216
  43.0 4.3 %collective-permute-start.1 = (bf16[144,256]{1,0:T(8,128)(2,1)S(1)}, bf16[144,256]{1,0:T(8,128)(2,1)S(1)}, u32[]{:S(2)}, u32[]{:S(2)}) collective-permute-start(bf16[144,256]{1,0:T(8,128)(2,1)S(1)} %get-tuple-element.11.refs_3_), channel_id=1, source_target_pairs={{0,4},{8,12},{16,20},{24,28},{32,36},{40,44},{48,52},{56,60},{64,6... | collective-permute-start | bytes 221192 | tf_op jit(solution)/shard_map/ppermute | solution.py:216

commit v8 on v7

--- a/solution.py
+++ b/solution.py
@@ -100,17 +100,15 @@
 
 def apply_to(transform, members):
     size = transform.shape[0]
-    pieces, rest = [], transform
-    for _ in range(3):
-        pieces.append(rest.astype(BF))
-        rest = rest - pieces[-1].astype(F32)
-    line = lax.broadcasted_iota(jnp.int32, (16, 3 * size), 0)
-    lane = lax.broadcasted_iota(jnp.int32, (16, 3 * size), 1)
+    high, low = split(transform)
+    held = high.astype(F32) + low.astype(F32)
+    line = lax.broadcasted_iota(jnp.int32, (16, 2 * size), 0)
+    lane = lax.broadcasted_iota(jnp.int32, (16, 2 * size), 1)
     ones = jnp.where(jnp.logical_and(line == 0, lane < size), 1.0, 0.0).astype(BF)
-    left = jnp.concatenate([jnp.concatenate(pieces, axis=1), ones], axis=0)
-    product = dot(left, jnp.concatenate([members] * 3, axis=0))
+    left = jnp.concatenate([jnp.concatenate([high, low], axis=1), ones], axis=0)
+    product = dot(left, jnp.concatenate([members] * 2, axis=0))
     average = product[size : size + 1] * (1.0 / size)
-    return (product[:size] - jnp.sum(transform, axis=1, keepdims=True) * average).astype(BF)
+    return (product[:size] - jnp.sum(held, axis=1, keepdims=True) * average).astype(BF)
 
 
 def is_even():

time: 84.8 us -> 84.7 us (level)
  no operation moved by 1% of the time
where the time goes in v8:
time: 84.7 us; the launch traced here: 84.3 us
  blocking collectives  34.4 us (41%)
  waiting for transfers between devices  27.1 us (32%)
  starting transfers between devices  15.2 us (18%)
  Pallas kernels  5.14 us (6%)
  local copies, waits for them, and re-layouts  2.28 us (3%)
    all_to_all x1, blocking collectives, on_device(): lax.all_to_all(outgoing, 'mem', split_axis=1, concat_axis=1, tiled=True)  34.4 us
    all_to_all x1, waiting for transfers between devices, on_device(): lax.all_to_all(ensemble, 'mem', split_axis=1, concat_axis=1, tiled=True)  27.1 us
    all_to_all x1, starting transfers between devices, on_device(): lax.all_to_all(ensemble, 'mem', split_axis=1, concat_axis=1, tiled=True)  13.1 us
    pallas_call x3, Pallas kernels, call(): pl.pallas_call(kernel, out_shape=out_shape, in_specs=[VMEM] * len(args),...  5.14 us
    unnamed x9, local copies, waits for them, and re-layouts  2.28 us
  transfers between devices with their start and end apart: 3, of which 1 were waited for; matrix products, arithmetic and copies ran while one was open for 0% of the time, Pallas kernels for 4%

profile of v8, /device:TPU:1, one launch (start us, length us, event | category | flops | bytes accessed | tf_op | source)
XLA Modules:
  0.0 84.3 jit_solution(1194754388356508418)
XLA Ops:
  0.0 0.0 copy-start
  0.0 13.1 %all-to-all-start = ((bf16[2,64,4096]{2,0,1:T(2,128)(2,1)}), bf16[2,64,4096]{2,0,1:T(2,128)(2,1)S(1)}, u32[]{:S(2)}, u32[]{:S(2)}) async-start(bf16[2,64,4096]{2,0,1:T(2,128)(2,1)} %bitcast.14), calls=%async_computation | async-start | bytes 2097152 | tf_op jit(solution)/shard_map/all_to_all | solution.py:220
  13.1 0.0 copy-done
  13.1 0.0 copy-start.1
  13.2 0.0 copy-start.3
  13.2 0.7 copy-done.1
  13.8 0.0 copy-done.3
  13.8 0.0 copy-start.2
  13.8 0.1 bitcast_select_fusion
  13.9 0.6 copy-done.2
  14.5 27.1 %all-to-all-done = bf16[2,64,4096]{2,0,1:T(2,128)(2,1)S(1)} async-done(((bf16[2,64,4096]{2,0,1:T(2,128)(2,1)}), bf16[2,64,4096]{2,0,1:T(2,128)(2,1)S(1)}, u32[]{:S(2)}, u32[]{:S(2)}) %all-to-all-start) | async-done | bytes 1048608 | tf_op jit(solution)/shard_map/all_to_all | solution.py:220
  41.7 0.3 shard_map.55
  42.0 1.0 %collective-permute-start = (bf16[144,256]{1,0:T(8,128)(2,1)S(1)}, bf16[144,256]{1,0:T(8,128)(2,1)S(1)}, u32[]{:S(2)}, u32[]{:S(2)}) collective-permute-start(bf16[144,256]{1,0:T(8,128)(2,1)S(1)} %get-tuple-element.10.refs_2_), channel_id=1, source_target_pairs={{4,8},{12,16},{20,24},{28,32},{36,40},{44,48},{52,56},{60,64},{68,... | collective-permute-start | bytes 221192 | tf_op jit(solution)/shard_map/ppermute | solution.py:214
  43.0 1.1 %collective-permute-start.1 = (bf16[144,256]{1,0:T(8,128)(2,1)S(1)}, bf16[144,256]{1,0:T(8,128)(2,1)S(1)}, u32[]{:S(2)}, u32[]{:S(2)}) collective-permute-start(bf16[144,256]{1,0:T(8,128)(2,1)S(1)} %get-tuple-element.11.refs_3_), channel_id=1, source_target_pairs={{0,4},{8,12},{16,20},{24,28},{32,36},{40,44},{48,52},{56,60},{64,6... | collective-permute-start | bytes 221192 | tf_op jit(solution)/shard_map/ppermute | solution.py:214
  44.1 3.0 %shard_map.56 = (bf16[64,2,3072]{2,1,0:T(2,128)(2,1)S(1)}, f32[2,144,128]{2,1,0:T(8,128)S(1)}, bf16[2,128,512]{2,1,0:T(8,128)(2,1)S(1)}) custom-call(bf16[64,2,4096]{2,1,0:T(2,128)(2,1)S(1)} %bitcast.11, f32[24,256]{1,0:T(8,128)S(1)} %pad_maximum_fusion.refs_1_, bf16[144,256]{1,0:T(8,128)(2,1)S(1)} %get-tuple-element.10.refs_2_, ...), custom_call_target="tpu_custom_call" | custom-call | flops 5000000000 | bytes 1220608 | tf_op jit(solution)/shard_map/pallas_call | solution.py:176
  47.2 0.0 collective-permute-done.refs_2_
  47.2 0.0 collective-permute-done.1.refs_3_
  47.2 1.8 %shard_map.57 = bf16[64,2,4096]{2,1,0:T(2,128)(2,1)S(1)} custom-call(bf16[2,128,512]{2,1,0:T(8,128)(2,1)S(1)} %get-tuple-element.12.refs_0_, f32[2,144,128]{2,1,0:T(8,128)S(1)} %get-tuple-element.13.refs_1_, bf16[144,256]{1,0:T(8,128)(2,1)S(1)} %collective-permute-done.refs_2_, bf16[144,256]{1,0:T(8,128)(2,1)S(1)} %collective-permute-done.1.refs_3_, ...), custom_call_target="tpu_custom_call" | custom-call | flops 2000000000 | bytes 1343488 | tf_op jit(solution)/shard_map/pallas_call | solution.py:176
  49.0 34.4 %all_to_all.18 = bf16[2,64,4096]{2,0,1:T(2,128)(2,1)S(1)} all-to-all(bf16[2,64,4096]{2,0,1:T(2,128)(2,1)S(1)} %bitcast.12), channel_id=1, replica_groups=mesh['mem'=64,'blk'=4] {'mem'}, dimensions={1} | all-to-all | bytes 2097152 | tf_op jit(solution)/shard_map/all_to_all | solution.py:225
  83.4 1.0 %copy.7 = bf16[2,262144]{1,0:T(2,128)(2,1)} copy(bf16[2,262144]{1,0:T(2,128)(2,1)S(1)} %bitcast.13) | data formatting | bytes 2097152
  (2 shorter events, 0.0 us)
Async XLA Ops:
  0.0 13.1 %copy-start = (s32[1,8,256]{2,1,0:T(8,128)S(1)}, s32[1,8,256]{2,1,0:T(8,128)}, u32[]{:S(2)}) copy-start(s32[1,8,256]{2,1,0:T(8,128)} %param.6) | copy-start | bytes 24580
  0.0 41.7 %all-to-all-start = ((bf16[2,64,4096]{2,0,1:T(2,128)(2,1)}), bf16[2,64,4096]{2,0,1:T(2,128)(2,1)S(1)}, u32[]{:S(2)}, u32[]{:S(2)}) async-start(bf16[2,64,4096]{2,0,1:T(2,128)(2,1)} %bitcast.14), calls=%async_computation | async-start | bytes 2097152 | tf_op jit(solution)/shard_map/all_to_all | solution.py:220
  13.1 0.7 copy-start.1
  13.2 0.7 copy-start.3
  13.8 0.7 copy-start.2
  42.0 5.2 %collective-permute-start = (bf16[144,256]{1,0:T(8,128)(2,1)S(1)}, bf16[144,256]{1,0:T(8,128)(2,1)S(1)}, u32[]{:S(2)}, u32[]{:S(2)}) collective-permute-start(bf16[144,256]{1,0:T(8,128)(2,1)S(1)} %get-tuple-element.10.refs_2_), channel_id=1, source_target_pairs={{4,8},{12,16},{20,24},{28,32},{36,40},{44,48},{52,56},{60,64},{68,... | collective-permute-start | bytes 221192 | tf_op jit(solution)/shard_map/ppermute | solution.py:214
  43.0 4.1 %collective-permute-start.1 = (bf16[144,256]{1,0:T(8,128)(2,1)S(1)}, bf16[144,256]{1,0:T(8,128)(2,1)S(1)}, u32[]{:S(2)}, u32[]{:S(2)}) collective-permute-start(bf16[144,256]{1,0:T(8,128)(2,1)S(1)} %get-tuple-element.11.refs_3_), channel_id=1, source_target_pairs={{0,4},{8,12},{16,20},{24,28},{32,36},{40,44},{48,52},{56,60},{64,6... | collective-permute-start | bytes 221192 | tf_op jit(solution)/shard_map/ppermute | solution.py:214

commit v9 on v8

--- a/solution.py
+++ b/solution.py
@@ -89,11 +89,13 @@
             y = [a[:size] for a in both]
             z = [a[size:] for a in both]
         else:
+            columns = [jnp.sum(eye * f, axis=1, keepdims=True) for f in forcings]
+            early = [jnp.sum(a * c, axis=0, keepdims=True) for a, c in zip(z, columns)]
+            inner = [jnp.sum(b * e, axis=1, keepdims=True) for b, e in zip(u, early)]
             z = [dot(left_of(a), right_of(b)) for a, b in zip(z, u)]
     out = []
-    for a, f, s in zip(z, forcings, scales):
-        inner = jnp.sum(a * f, axis=1, keepdims=True)
-        weights = jnp.sum(a * inner, axis=0, keepdims=True) * s
+    for a, i, s in zip(z, inner, scales):
+        weights = jnp.sum(a * i, axis=0, keepdims=True) * s
         out.append(jnp.sqrt(s * (size - 1.0)) * a + weights - eye)
     return out
 

time: 84.7 us -> 84.6 us (level)
  no operation moved by 1% of the time
where the time goes in v9:
time: 84.6 us; the launch traced here: 84.2 us
  blocking collectives  34.4 us (41%)
  waiting for transfers between devices  27.1 us (32%)
  starting transfers between devices  15.2 us (18%)
  Pallas kernels  4.99 us (6%)
  local copies, waits for them, and re-layouts  2.28 us (3%)
    all_to_all x1, blocking collectives, on_device(): lax.all_to_all(outgoing, 'mem', split_axis=1, concat_axis=1, tiled=True)  34.4 us
    all_to_all x1, waiting for transfers between devices, on_device(): lax.all_to_all(ensemble, 'mem', split_axis=1, concat_axis=1, tiled=True)  27.1 us
    all_to_all x1, starting transfers between devices, on_device(): lax.all_to_all(ensemble, 'mem', split_axis=1, concat_axis=1, tiled=True)  13.1 us
    pallas_call x3, Pallas kernels, call(): pl.pallas_call(kernel, out_shape=out_shape, in_specs=[VMEM] * len(args),...  4.99 us
    unnamed x9, local copies, waits for them, and re-layouts  2.28 us
  transfers between devices with their start and end apart: 3, of which 1 were waited for; matrix products, arithmetic and copies ran while one was open for 0% of the time, Pallas kernels for 4%

profile of v9, /device:TPU:1, one launch (start us, length us, event | category | flops | bytes accessed | tf_op | source)
XLA Modules:
  0.0 84.2 jit_solution(7344790113054088905)
XLA Ops:
  0.0 0.0 copy-start
  0.0 13.1 %all-to-all-start = ((bf16[2,64,4096]{2,0,1:T(2,128)(2,1)}), bf16[2,64,4096]{2,0,1:T(2,128)(2,1)S(1)}, u32[]{:S(2)}, u32[]{:S(2)}) async-start(bf16[2,64,4096]{2,0,1:T(2,128)(2,1)} %bitcast.14), calls=%async_computation | async-start | bytes 2097152 | tf_op jit(solution)/shard_map/all_to_all | solution.py:222
  13.1 0.0 copy-done
  13.1 0.0 copy-start.1
  13.2 0.0 copy-start.3
  13.2 0.7 copy-done.1
  13.8 0.0 copy-done.3
  13.8 0.0 copy-start.2
  13.8 0.1 bitcast_select_fusion
  13.9 0.6 copy-done.2
  14.5 27.1 %all-to-all-done = bf16[2,64,4096]{2,0,1:T(2,128)(2,1)S(1)} async-done(((bf16[2,64,4096]{2,0,1:T(2,128)(2,1)}), bf16[2,64,4096]{2,0,1:T(2,128)(2,1)S(1)}, u32[]{:S(2)}, u32[]{:S(2)}) %all-to-all-start) | async-done | bytes 1048608 | tf_op jit(solution)/shard_map/all_to_all | solution.py:222
  41.7 0.3 shard_map.55
  42.0 1.0 %collective-permute-start = (bf16[144,256]{1,0:T(8,128)(2,1)S(1)}, bf16[144,256]{1,0:T(8,128)(2,1)S(1)}, u32[]{:S(2)}, u32[]{:S(2)}) collective-permute-start(bf16[144,256]{1,0:T(8,128)(2,1)S(1)} %get-tuple-element.10.refs_2_), channel_id=1, source_target_pairs={{4,8},{12,16},{20,24},{28,32},{36,40},{44,48},{52,56},{60,64},{68,... | collective-permute-start | bytes 221192 | tf_op jit(solution)/shard_map/ppermute | solution.py:216
  43.0 1.1 %collective-permute-start.1 = (bf16[144,256]{1,0:T(8,128)(2,1)S(1)}, bf16[144,256]{1,0:T(8,128)(2,1)S(1)}, u32[]{:S(2)}, u32[]{:S(2)}) collective-permute-start(bf16[144,256]{1,0:T(8,128)(2,1)S(1)} %get-tuple-element.11.refs_3_), channel_id=1, source_target_pairs={{0,4},{8,12},{16,20},{24,28},{32,36},{40,44},{48,52},{56,60},{64,6... | collective-permute-start | bytes 221192 | tf_op jit(solution)/shard_map/ppermute | solution.py:216
  44.1 3.0 %shard_map.56 = (bf16[64,2,3072]{2,1,0:T(2,128)(2,1)S(1)}, f32[2,144,128]{2,1,0:T(8,128)S(1)}, bf16[2,128,512]{2,1,0:T(8,128)(2,1)S(1)}) custom-call(bf16[64,2,4096]{2,1,0:T(2,128)(2,1)S(1)} %bitcast.11, f32[24,256]{1,0:T(8,128)S(1)} %pad_maximum_fusion.refs_1_, bf16[144,256]{1,0:T(8,128)(2,1)S(1)} %get-tuple-element.10.refs_2_, ...), custom_call_target="tpu_custom_call" | custom-call | flops 5000000000 | bytes 1220608 | tf_op jit(solution)/shard_map/pallas_call | solution.py:178
  47.1 0.0 collective-permute-done.refs_2_
  47.1 0.0 collective-permute-done.1.refs_3_
  47.1 1.7 %shard_map.57 = bf16[64,2,4096]{2,1,0:T(2,128)(2,1)S(1)} custom-call(bf16[2,128,512]{2,1,0:T(8,128)(2,1)S(1)} %get-tuple-element.12.refs_0_, f32[2,144,128]{2,1,0:T(8,128)S(1)} %get-tuple-element.13.refs_1_, bf16[144,256]{1,0:T(8,128)(2,1)S(1)} %collective-permute-done.refs_2_, bf16[144,256]{1,0:T(8,128)(2,1)S(1)} %collective-permute-done.1.refs_3_, ...), custom_call_target="tpu_custom_call" | custom-call | flops 2000000000 | bytes 1343488 | tf_op jit(solution)/shard_map/pallas_call | solution.py:178
  48.8 34.4 %all_to_all.18 = bf16[2,64,4096]{2,0,1:T(2,128)(2,1)S(1)} all-to-all(bf16[2,64,4096]{2,0,1:T(2,128)(2,1)S(1)} %bitcast.12), channel_id=1, replica_groups=mesh['mem'=64,'blk'=4] {'mem'}, dimensions={1} | all-to-all | bytes 2097152 | tf_op jit(solution)/shard_map/all_to_all | solution.py:227
  83.3 1.0 %copy.7 = bf16[2,262144]{1,0:T(2,128)(2,1)} copy(bf16[2,262144]{1,0:T(2,128)(2,1)S(1)} %bitcast.13) | data formatting | bytes 2097152
  (2 shorter events, 0.0 us)
Async XLA Ops:
  0.0 13.1 %copy-start = (s32[1,8,256]{2,1,0:T(8,128)S(1)}, s32[1,8,256]{2,1,0:T(8,128)}, u32[]{:S(2)}) copy-start(s32[1,8,256]{2,1,0:T(8,128)} %param.6) | copy-start | bytes 24580
  0.0 41.7 %all-to-all-start = ((bf16[2,64,4096]{2,0,1:T(2,128)(2,1)}), bf16[2,64,4096]{2,0,1:T(2,128)(2,1)S(1)}, u32[]{:S(2)}, u32[]{:S(2)}) async-start(bf16[2,64,4096]{2,0,1:T(2,128)(2,1)} %bitcast.14), calls=%async_computation | async-start | bytes 2097152 | tf_op jit(solution)/shard_map/all_to_all | solution.py:222
  13.1 0.7 copy-start.1
  13.2 0.7 copy-start.3
  13.8 0.7 copy-start.2
  42.0 5.1 %collective-permute-start = (bf16[144,256]{1,0:T(8,128)(2,1)S(1)}, bf16[144,256]{1,0:T(8,128)(2,1)S(1)}, u32[]{:S(2)}, u32[]{:S(2)}) collective-permute-start(bf16[144,256]{1,0:T(8,128)(2,1)S(1)} %get-tuple-element.10.refs_2_), channel_id=1, source_target_pairs={{4,8},{12,16},{20,24},{28,32},{36,40},{44,48},{52,56},{60,64},{68,... | collective-permute-start | bytes 221192 | tf_op jit(solution)/shard_map/ppermute | solution.py:216
  43.0 4.1 %collective-permute-start.1 = (bf16[144,256]{1,0:T(8,128)(2,1)S(1)}, bf16[144,256]{1,0:T(8,128)(2,1)S(1)}, u32[]{:S(2)}, u32[]{:S(2)}) collective-permute-start(bf16[144,256]{1,0:T(8,128)(2,1)S(1)} %get-tuple-element.11.refs_3_), channel_id=1, source_target_pairs={{0,4},{8,12},{16,20},{24,28},{32,36},{40,44},{48,52},{56,60},{64,6... | collective-permute-start | bytes 221192 | tf_op jit(solution)/shard_map/ppermute | solution.py:216

commit v10 on v9

--- a/solution.py
+++ b/solution.py
@@ -11,7 +11,7 @@
 
 BF = jnp.bfloat16
 F32 = jnp.float32
-ROWS = 144
+ROWS = 136
 
 
 def split(a):

time: 84.6 us -> 84.6 us (level)
  no operation moved by 1% of the time
where the time goes in v10:
time: 84.6 us; the launch traced here: 84.2 us
  blocking collectives  34.4 us (41%)
  waiting for transfers between devices  27.1 us (32%)
  starting transfers between devices  15.2 us (18%)
  Pallas kernels  4.98 us (6%)
  local copies, waits for them, and re-layouts  2.28 us (3%)
    all_to_all x1, blocking collectives, on_device(): lax.all_to_all(outgoing, 'mem', split_axis=1, concat_axis=1, tiled=True)  34.4 us
    all_to_all x1, waiting for transfers between devices, on_device(): lax.all_to_all(ensemble, 'mem', split_axis=1, concat_axis=1, tiled=True)  27.1 us
    all_to_all x1, starting transfers between devices, on_device(): lax.all_to_all(ensemble, 'mem', split_axis=1, concat_axis=1, tiled=True)  13.1 us
    pallas_call x3, Pallas kernels, call(): pl.pallas_call(kernel, out_shape=out_shape, in_specs=[VMEM] * len(args),...  4.98 us
    unnamed x9, local copies, waits for them, and re-layouts  2.28 us
  transfers between devices with their start and end apart: 3, of which 1 were waited for; matrix products, arithmetic and copies ran while one was open for 0% of the time, Pallas kernels for 4%

profile of v10, /device:TPU:1, one launch (start us, length us, event | category | flops | bytes accessed | tf_op | source)
XLA Modules:
  0.0 84.2 jit_solution(14946898517347239744)
XLA Ops:
  0.0 0.0 copy-start
  0.0 13.1 %all-to-all-start = ((bf16[2,64,4096]{2,0,1:T(2,128)(2,1)}), bf16[2,64,4096]{2,0,1:T(2,128)(2,1)S(1)}, u32[]{:S(2)}, u32[]{:S(2)}) async-start(bf16[2,64,4096]{2,0,1:T(2,128)(2,1)} %bitcast.14), calls=%async_computation | async-start | bytes 2097152 | tf_op jit(solution)/shard_map/all_to_all | solution.py:222
  13.1 0.0 copy-done
  13.1 0.0 copy-start.1
  13.2 0.0 copy-start.3
  13.2 0.7 copy-done.1
  13.8 0.0 copy-done.3
  13.8 0.0 copy-start.2
  13.8 0.1 bitcast_select_fusion
  13.9 0.6 copy-done.2
  14.5 27.1 %all-to-all-done = bf16[2,64,4096]{2,0,1:T(2,128)(2,1)S(1)} async-done(((bf16[2,64,4096]{2,0,1:T(2,128)(2,1)}), bf16[2,64,4096]{2,0,1:T(2,128)(2,1)S(1)}, u32[]{:S(2)}, u32[]{:S(2)}) %all-to-all-start) | async-done | bytes 1048608 | tf_op jit(solution)/shard_map/all_to_all | solution.py:222
  41.7 0.3 shard_map.55
  42.0 1.0 %collective-permute-start = (bf16[136,256]{1,0:T(8,128)(2,1)S(1)}, bf16[136,256]{1,0:T(8,128)(2,1)S(1)}, u32[]{:S(2)}, u32[]{:S(2)}) collective-permute-start(bf16[136,256]{1,0:T(8,128)(2,1)S(1)} %get-tuple-element.10.refs_2_), channel_id=1, source_target_pairs={{4,8},{12,16},{20,24},{28,32},{36,40},{44,48},{52,56},{60,64},{68,... | collective-permute-start | bytes 208904 | tf_op jit(solution)/shard_map/ppermute | solution.py:216
  43.0 1.1 %collective-permute-start.1 = (bf16[136,256]{1,0:T(8,128)(2,1)S(1)}, bf16[136,256]{1,0:T(8,128)(2,1)S(1)}, u32[]{:S(2)}, u32[]{:S(2)}) collective-permute-start(bf16[136,256]{1,0:T(8,128)(2,1)S(1)} %get-tuple-element.11.refs_3_), channel_id=1, source_target_pairs={{0,4},{8,12},{16,20},{24,28},{32,36},{40,44},{48,52},{56,60},{64,6... | collective-permute-start | bytes 208904 | tf_op jit(solution)/shard_map/ppermute | solution.py:216
  44.1 3.0 %shard_map.56 = (bf16[64,2,3072]{2,1,0:T(2,128)(2,1)S(1)}, f32[2,136,128]{2,1,0:T(8,128)S(1)}, bf16[2,128,512]{2,1,0:T(8,128)(2,1)S(1)}) custom-call(bf16[64,2,4096]{2,1,0:T(2,128)(2,1)S(1)} %bitcast.11, f32[24,256]{1,0:T(8,128)S(1)} %pad_maximum_fusion.refs_1_, bf16[136,256]{1,0:T(8,128)(2,1)S(1)} %get-tuple-element.10.refs_2_, ...), custom_call_target="tpu_custom_call" | custom-call | flops 5000000000 | bytes 1212416 | tf_op jit(solution)/shard_map/pallas_call | solution.py:178
  47.1 0.0 collective-permute-done.refs_2_
  47.1 0.0 collective-permute-done.1.refs_3_
  47.1 1.7 %shard_map.57 = bf16[64,2,4096]{2,1,0:T(2,128)(2,1)S(1)} custom-call(bf16[2,128,512]{2,1,0:T(8,128)(2,1)S(1)} %get-tuple-element.12.refs_0_, f32[2,136,128]{2,1,0:T(8,128)S(1)} %get-tuple-element.13.refs_1_, bf16[136,256]{1,0:T(8,128)(2,1)S(1)} %collective-permute-done.refs_2_, bf16[136,256]{1,0:T(8,128)(2,1)S(1)} %collective-permute-done.1.refs_3_, ...), custom_call_target="tpu_custom_call" | custom-call | flops 2000000000 | bytes 1327104 | tf_op jit(solution)/shard_map/pallas_call | solution.py:178
  48.8 34.4 %all_to_all.18 = bf16[2,64,4096]{2,0,1:T(2,128)(2,1)S(1)} all-to-all(bf16[2,64,4096]{2,0,1:T(2,128)(2,1)S(1)} %bitcast.12), channel_id=1, replica_groups=mesh['mem'=64,'blk'=4] {'mem'}, dimensions={1} | all-to-all | bytes 2097152 | tf_op jit(solution)/shard_map/all_to_all | solution.py:227
  83.2 1.0 %copy.7 = bf16[2,262144]{1,0:T(2,128)(2,1)} copy(bf16[2,262144]{1,0:T(2,128)(2,1)S(1)} %bitcast.13) | data formatting | bytes 2097152
  (2 shorter events, 0.0 us)
Async XLA Ops:
  0.0 13.1 %copy-start = (s32[1,8,256]{2,1,0:T(8,128)S(1)}, s32[1,8,256]{2,1,0:T(8,128)}, u32[]{:S(2)}) copy-start(s32[1,8,256]{2,1,0:T(8,128)} %param.6) | copy-start | bytes 24580
  0.0 41.7 %all-to-all-start = ((bf16[2,64,4096]{2,0,1:T(2,128)(2,1)}), bf16[2,64,4096]{2,0,1:T(2,128)(2,1)S(1)}, u32[]{:S(2)}, u32[]{:S(2)}) async-start(bf16[2,64,4096]{2,0,1:T(2,128)(2,1)} %bitcast.14), calls=%async_computation | async-start | bytes 2097152 | tf_op jit(solution)/shard_map/all_to_all | solution.py:222
  13.1 0.7 copy-start.1
  13.2 0.7 copy-start.3
  13.8 0.7 copy-start.2
  42.0 5.1 %collective-permute-start = (bf16[136,256]{1,0:T(8,128)(2,1)S(1)}, bf16[136,256]{1,0:T(8,128)(2,1)S(1)}, u32[]{:S(2)}, u32[]{:S(2)}) collective-permute-start(bf16[136,256]{1,0:T(8,128)(2,1)S(1)} %get-tuple-element.10.refs_2_), channel_id=1, source_target_pairs={{4,8},{12,16},{20,24},{28,32},{36,40},{44,48},{52,56},{60,64},{68,... | collective-permute-start | bytes 208904 | tf_op jit(solution)/shard_map/ppermute | solution.py:216
  43.0 4.1 %collective-permute-start.1 = (bf16[136,256]{1,0:T(8,128)(2,1)S(1)}, bf16[136,256]{1,0:T(8,128)(2,1)S(1)}, u32[]{:S(2)}, u32[]{:S(2)}) collective-permute-start(bf16[136,256]{1,0:T(8,128)(2,1)S(1)} %get-tuple-element.11.refs_3_), channel_id=1, source_target_pairs={{0,4},{8,12},{16,20},{24,28},{32,36},{40,44},{48,52},{56,60},{64,6... | collective-permute-start | bytes 208904 | tf_op jit(solution)/shard_map/ppermute | solution.py:216

commit v11 on v10

--- a/solution.py
+++ b/solution.py
@@ -104,8 +104,8 @@
     size = transform.shape[0]
     high, low = split(transform)
     held = high.astype(F32) + low.astype(F32)
-    line = lax.broadcasted_iota(jnp.int32, (16, 2 * size), 0)
-    lane = lax.broadcasted_iota(jnp.int32, (16, 2 * size), 1)
+    line = lax.broadcasted_iota(jnp.int32, (8, 2 * size), 0)
+    lane = lax.broadcasted_iota(jnp.int32, (8, 2 * size), 1)
     ones = jnp.where(jnp.logical_and(line == 0, lane < size), 1.0, 0.0).astype(BF)
     left = jnp.concatenate([jnp.concatenate([high, low], axis=1), ones], axis=0)
     product = dot(left, jnp.concatenate([members] * 2, axis=0))

time: 84.6 us -> 84.6 us (level)
  no operation moved by 1% of the time
where the time goes in v11:
time: 84.6 us; the launch traced here: 84.2 us
  blocking collectives  34.4 us (41%)
  waiting for transfers between devices  27.1 us (32%)
  starting transfers between devices  15.2 us (18%)
  Pallas kernels  4.99 us (6%)
  local copies, waits for them, and re-layouts  2.28 us (3%)
    all_to_all x1, blocking collectives, on_device(): lax.all_to_all(outgoing, 'mem', split_axis=1, concat_axis=1, tiled=True)  34.4 us
    all_to_all x1, waiting for transfers between devices, on_device(): lax.all_to_all(ensemble, 'mem', split_axis=1, concat_axis=1, tiled=True)  27.1 us
    all_to_all x1, starting transfers between devices, on_device(): lax.all_to_all(ensemble, 'mem', split_axis=1, concat_axis=1, tiled=True)  13.1 us
    pallas_call x3, Pallas kernels, call(): pl.pallas_call(kernel, out_shape=out_shape, in_specs=[VMEM] * len(args),...  4.99 us
    unnamed x9, local copies, waits for them, and re-layouts  2.28 us
  transfers between devices with their start and end apart: 3, of which 1 were waited for; matrix products, arithmetic and copies ran while one was open for 0% of the time, Pallas kernels for 4%

profile of v11, /device:TPU:1, one launch (start us, length us, event | category | flops | bytes accessed | tf_op | source)
XLA Modules:
  0.0 84.2 jit_solution(5430447522507295537)
XLA Ops:
  0.0 0.0 copy-start
  0.0 13.1 %all-to-all-start = ((bf16[2,64,4096]{2,0,1:T(2,128)(2,1)}), bf16[2,64,4096]{2,0,1:T(2,128)(2,1)S(1)}, u32[]{:S(2)}, u32[]{:S(2)}) async-start(bf16[2,64,4096]{2,0,1:T(2,128)(2,1)} %bitcast.14), calls=%async_computation | async-start | bytes 2097152 | tf_op jit(solution)/shard_map/all_to_all | solution.py:222
  13.1 0.0 copy-done
  13.1 0.0 copy-start.1
  13.2 0.0 copy-start.3
  13.2 0.7 copy-done.1
  13.8 0.0 copy-done.3
  13.8 0.0 copy-start.2
  13.8 0.1 bitcast_select_fusion
  13.9 0.6 copy-done.2
  14.5 27.1 %all-to-all-done = bf16[2,64,4096]{2,0,1:T(2,128)(2,1)S(1)} async-done(((bf16[2,64,4096]{2,0,1:T(2,128)(2,1)}), bf16[2,64,4096]{2,0,1:T(2,128)(2,1)S(1)}, u32[]{:S(2)}, u32[]{:S(2)}) %all-to-all-start) | async-done | bytes 1048608 | tf_op jit(solution)/shard_map/all_to_all | solution.py:222
  41.7 0.3 shard_map.55
  42.0 1.0 %collective-permute-start = (bf16[136,256]{1,0:T(8,128)(2,1)S(1)}, bf16[136,256]{1,0:T(8,128)(2,1)S(1)}, u32[]{:S(2)}, u32[]{:S(2)}) collective-permute-start(bf16[136,256]{1,0:T(8,128)(2,1)S(1)} %get-tuple-element.10.refs_2_), channel_id=1, source_target_pairs={{4,8},{12,16},{20,24},{28,32},{36,40},{44,48},{52,56},{60,64},{68,... | collective-permute-start | bytes 208904 | tf_op jit(solution)/shard_map/ppermute | solution.py:216
  43.0 1.1 %collective-permute-start.1 = (bf16[136,256]{1,0:T(8,128)(2,1)S(1)}, bf16[136,256]{1,0:T(8,128)(2,1)S(1)}, u32[]{:S(2)}, u32[]{:S(2)}) collective-permute-start(bf16[136,256]{1,0:T(8,128)(2,1)S(1)} %get-tuple-element.11.refs_3_), channel_id=1, source_target_pairs={{0,4},{8,12},{16,20},{24,28},{32,36},{40,44},{48,52},{56,60},{64,6... | collective-permute-start | bytes 208904 | tf_op jit(solution)/shard_map/ppermute | solution.py:216
  44.1 3.0 %shard_map.56 = (bf16[64,2,3072]{2,1,0:T(2,128)(2,1)S(1)}, f32[2,136,128]{2,1,0:T(8,128)S(1)}, bf16[2,128,512]{2,1,0:T(8,128)(2,1)S(1)}) custom-call(bf16[64,2,4096]{2,1,0:T(2,128)(2,1)S(1)} %bitcast.11, f32[24,256]{1,0:T(8,128)S(1)} %pad_maximum_fusion.refs_1_, bf16[136,256]{1,0:T(8,128)(2,1)S(1)} %get-tuple-element.10.refs_2_, ...), custom_call_target="tpu_custom_call" | custom-call | flops 5000000000 | bytes 1212416 | tf_op jit(solution)/shard_map/pallas_call | solution.py:178
  47.1 0.0 collective-permute-done.refs_2_
  47.1 0.0 collective-permute-done.1.refs_3_
  47.1 1.7 %shard_map.57 = bf16[64,2,4096]{2,1,0:T(2,128)(2,1)S(1)} custom-call(bf16[2,128,512]{2,1,0:T(8,128)(2,1)S(1)} %get-tuple-element.12.refs_0_, f32[2,136,128]{2,1,0:T(8,128)S(1)} %get-tuple-element.13.refs_1_, bf16[136,256]{1,0:T(8,128)(2,1)S(1)} %collective-permute-done.refs_2_, bf16[136,256]{1,0:T(8,128)(2,1)S(1)} %collective-permute-done.1.refs_3_, ...), custom_call_target="tpu_custom_call" | custom-call | flops 2000000000 | bytes 1327104 | tf_op jit(solution)/shard_map/pallas_call | solution.py:178
  48.8 34.4 %all_to_all.18 = bf16[2,64,4096]{2,0,1:T(2,128)(2,1)S(1)} all-to-all(bf16[2,64,4096]{2,0,1:T(2,128)(2,1)S(1)} %bitcast.12), channel_id=1, replica_groups=mesh['mem'=64,'blk'=4] {'mem'}, dimensions={1} | all-to-all | bytes 2097152 | tf_op jit(solution)/shard_map/all_to_all | solution.py:227
  83.2 1.0 %copy.7 = bf16[2,262144]{1,0:T(2,128)(2,1)} copy(bf16[2,262144]{1,0:T(2,128)(2,1)S(1)} %bitcast.13) | data formatting | bytes 2097152
  (2 shorter events, 0.0 us)
Async XLA Ops:
  0.0 13.1 %copy-start = (s32[1,8,256]{2,1,0:T(8,128)S(1)}, s32[1,8,256]{2,1,0:T(8,128)}, u32[]{:S(2)}) copy-start(s32[1,8,256]{2,1,0:T(8,128)} %param.6) | copy-start | bytes 24580
  0.0 41.7 %all-to-all-start = ((bf16[2,64,4096]{2,0,1:T(2,128)(2,1)}), bf16[2,64,4096]{2,0,1:T(2,128)(2,1)S(1)}, u32[]{:S(2)}, u32[]{:S(2)}) async-start(bf16[2,64,4096]{2,0,1:T(2,128)(2,1)} %bitcast.14), calls=%async_computation | async-start | bytes 2097152 | tf_op jit(solution)/shard_map/all_to_all | solution.py:222
  13.1 0.7 copy-start.1
  13.2 0.7 copy-start.3
  13.8 0.7 copy-start.2
  42.0 5.1 %collective-permute-start = (bf16[136,256]{1,0:T(8,128)(2,1)S(1)}, bf16[136,256]{1,0:T(8,128)(2,1)S(1)}, u32[]{:S(2)}, u32[]{:S(2)}) collective-permute-start(bf16[136,256]{1,0:T(8,128)(2,1)S(1)} %get-tuple-element.10.refs_2_), channel_id=1, source_target_pairs={{4,8},{12,16},{20,24},{28,32},{36,40},{44,48},{52,56},{60,64},{68,... | collective-permute-start | bytes 208904 | tf_op jit(solution)/shard_map/ppermute | solution.py:216
  43.0 4.1 %collective-permute-start.1 = (bf16[136,256]{1,0:T(8,128)(2,1)S(1)}, bf16[136,256]{1,0:T(8,128)(2,1)S(1)}, u32[]{:S(2)}, u32[]{:S(2)}) collective-permute-start(bf16[136,256]{1,0:T(8,128)(2,1)S(1)} %get-tuple-element.11.refs_3_), channel_id=1, source_target_pairs={{0,4},{8,12},{16,20},{24,28},{32,36},{40,44},{48,52},{56,60},{64,6... | collective-permute-start | bytes 208904 | tf_op jit(solution)/shard_map/ppermute | solution.py:216

commit v12 on v10

--- a/solution.py
+++ b/solution.py
@@ -165,8 +165,8 @@
     width = edge_ref.shape[2]
     left, right = ordered(across_ref, partner_ref)
     localized = [part_ref[0] + localize * left, part_ref[1] + localize * right]
+    finish((0, blocks - 1), localized, [lambda: edge_ref[0], lambda: edge_ref[1]], out_ref)
     out_ref[:, :, width : (blocks - 1) * width] = inner_ref[...]
-    finish((0, blocks - 1), localized, [lambda: edge_ref[0], lambda: edge_ref[1]], out_ref)
 
 
 VMEM = pl.BlockSpec(memory_space=pltpu.VMEM)

time: 84.6 us -> 84.6 us (level)
  no operation moved by 1% of the time
where the time goes in v12:
time: 84.6 us; the launch traced here: 84.2 us
  blocking collectives  34.4 us (41%)
  waiting for transfers between devices  27.1 us (32%)
  starting transfers between devices  15.2 us (18%)
  Pallas kernels  5 us (6%)
  local copies, waits for them, and re-layouts  2.28 us (3%)
    all_to_all x1, blocking collectives, on_device(): lax.all_to_all(outgoing, 'mem', split_axis=1, concat_axis=1, tiled=True)  34.4 us
    all_to_all x1, waiting for transfers between devices, on_device(): lax.all_to_all(ensemble, 'mem', split_axis=1, concat_axis=1, tiled=True)  27.1 us
    all_to_all x1, starting transfers between devices, on_device(): lax.all_to_all(ensemble, 'mem', split_axis=1, concat_axis=1, tiled=True)  13.1 us
    pallas_call x3, Pallas kernels, call(): pl.pallas_call(kernel, out_shape=out_shape, in_specs=[VMEM] * len(args),...  5 us
    unnamed x9, local copies, waits for them, and re-layouts  2.28 us
  transfers between devices with their start and end apart: 3, of which 1 were waited for; matrix products, arithmetic and copies ran while one was open for 0% of the time, Pallas kernels for 4%

profile of v12, /device:TPU:1, one launch (start us, length us, event | category | flops | bytes accessed | tf_op | source)
XLA Modules:
  0.0 84.2 jit_solution(15339153579162134858)
XLA Ops:
  0.0 0.0 copy-start
  0.0 13.1 %all-to-all-start = ((bf16[2,64,4096]{2,0,1:T(2,128)(2,1)}), bf16[2,64,4096]{2,0,1:T(2,128)(2,1)S(1)}, u32[]{:S(2)}, u32[]{:S(2)}) async-start(bf16[2,64,4096]{2,0,1:T(2,128)(2,1)} %bitcast.14), calls=%async_computation | async-start | bytes 2097152 | tf_op jit(solution)/shard_map/all_to_all | solution.py:222
  13.1 0.0 copy-done
  13.1 0.0 copy-start.1
  13.2 0.0 copy-start.3
  13.2 0.7 copy-done.1
  13.8 0.0 copy-done.3
  13.8 0.0 copy-start.2
  13.8 0.1 bitcast_select_fusion
  13.9 0.6 copy-done.2
  14.5 27.1 %all-to-all-done = bf16[2,64,4096]{2,0,1:T(2,128)(2,1)S(1)} async-done(((bf16[2,64,4096]{2,0,1:T(2,128)(2,1)}), bf16[2,64,4096]{2,0,1:T(2,128)(2,1)S(1)}, u32[]{:S(2)}, u32[]{:S(2)}) %all-to-all-start) | async-done | bytes 1048608 | tf_op jit(solution)/shard_map/all_to_all | solution.py:222
  41.7 0.3 shard_map.55
  42.0 1.0 %collective-permute-start = (bf16[136,256]{1,0:T(8,128)(2,1)S(1)}, bf16[136,256]{1,0:T(8,128)(2,1)S(1)}, u32[]{:S(2)}, u32[]{:S(2)}) collective-permute-start(bf16[136,256]{1,0:T(8,128)(2,1)S(1)} %get-tuple-element.10.refs_2_), channel_id=1, source_target_pairs={{4,8},{12,16},{20,24},{28,32},{36,40},{44,48},{52,56},{60,64},{68,... | collective-permute-start | bytes 208904 | tf_op jit(solution)/shard_map/ppermute | solution.py:216
  43.0 1.1 %collective-permute-start.1 = (bf16[136,256]{1,0:T(8,128)(2,1)S(1)}, bf16[136,256]{1,0:T(8,128)(2,1)S(1)}, u32[]{:S(2)}, u32[]{:S(2)}) collective-permute-start(bf16[136,256]{1,0:T(8,128)(2,1)S(1)} %get-tuple-element.11.refs_3_), channel_id=1, source_target_pairs={{0,4},{8,12},{16,20},{24,28},{32,36},{40,44},{48,52},{56,60},{64,6... | collective-permute-start | bytes 208904 | tf_op jit(solution)/shard_map/ppermute | solution.py:216
  44.1 3.0 %shard_map.56 = (bf16[64,2,3072]{2,1,0:T(2,128)(2,1)S(1)}, f32[2,136,128]{2,1,0:T(8,128)S(1)}, bf16[2,128,512]{2,1,0:T(8,128)(2,1)S(1)}) custom-call(bf16[64,2,4096]{2,1,0:T(2,128)(2,1)S(1)} %bitcast.11, f32[24,256]{1,0:T(8,128)S(1)} %pad_maximum_fusion.refs_1_, bf16[136,256]{1,0:T(8,128)(2,1)S(1)} %get-tuple-element.10.refs_2_, ...), custom_call_target="tpu_custom_call" | custom-call | flops 5000000000 | bytes 1212416 | tf_op jit(solution)/shard_map/pallas_call | solution.py:178
  47.1 0.0 collective-permute-done.refs_2_
  47.1 0.0 collective-permute-done.1.refs_3_
  47.1 1.7 %shard_map.57 = bf16[64,2,4096]{2,1,0:T(2,128)(2,1)S(1)} custom-call(bf16[2,128,512]{2,1,0:T(8,128)(2,1)S(1)} %get-tuple-element.12.refs_0_, f32[2,136,128]{2,1,0:T(8,128)S(1)} %get-tuple-element.13.refs_1_, bf16[136,256]{1,0:T(8,128)(2,1)S(1)} %collective-permute-done.refs_2_, bf16[136,256]{1,0:T(8,128)(2,1)S(1)} %collective-permute-done.1.refs_3_, ...), custom_call_target="tpu_custom_call" | custom-call | flops 2000000000 | bytes 1327104 | tf_op jit(solution)/shard_map/pallas_call | solution.py:178
  48.8 34.4 %all_to_all.18 = bf16[2,64,4096]{2,0,1:T(2,128)(2,1)S(1)} all-to-all(bf16[2,64,4096]{2,0,1:T(2,128)(2,1)S(1)} %bitcast.12), channel_id=1, replica_groups=mesh['mem'=64,'blk'=4] {'mem'}, dimensions={1} | all-to-all | bytes 2097152 | tf_op jit(solution)/shard_map/all_to_all | solution.py:227
  83.2 1.0 %copy.7 = bf16[2,262144]{1,0:T(2,128)(2,1)} copy(bf16[2,262144]{1,0:T(2,128)(2,1)S(1)} %bitcast.13) | data formatting | bytes 2097152
  (2 shorter events, 0.0 us)
Async XLA Ops:
  0.0 13.1 %copy-start = (s32[1,8,256]{2,1,0:T(8,128)S(1)}, s32[1,8,256]{2,1,0:T(8,128)}, u32[]{:S(2)}) copy-start(s32[1,8,256]{2,1,0:T(8,128)} %param.6) | copy-start | bytes 24580
  0.0 41.7 %all-to-all-start = ((bf16[2,64,4096]{2,0,1:T(2,128)(2,1)}), bf16[2,64,4096]{2,0,1:T(2,128)(2,1)S(1)}, u32[]{:S(2)}, u32[]{:S(2)}) async-start(bf16[2,64,4096]{2,0,1:T(2,128)(2,1)} %bitcast.14), calls=%async_computation | async-start | bytes 2097152 | tf_op jit(solution)/shard_map/all_to_all | solution.py:222
  13.1 0.7 copy-start.1
  13.2 0.7 copy-start.3
  13.8 0.7 copy-start.2
  42.0 5.1 %collective-permute-start = (bf16[136,256]{1,0:T(8,128)(2,1)S(1)}, bf16[136,256]{1,0:T(8,128)(2,1)S(1)}, u32[]{:S(2)}, u32[]{:S(2)}) collective-permute-start(bf16[136,256]{1,0:T(8,128)(2,1)S(1)} %get-tuple-element.10.refs_2_), channel_id=1, source_target_pairs={{4,8},{12,16},{20,24},{28,32},{36,40},{44,48},{52,56},{60,64},{68,... | collective-permute-start | bytes 208904 | tf_op jit(solution)/shard_map/ppermute | solution.py:216
  43.0 4.1 %collective-permute-start.1 = (bf16[136,256]{1,0:T(8,128)(2,1)S(1)}, bf16[136,256]{1,0:T(8,128)(2,1)S(1)}, u32[]{:S(2)}, u32[]{:S(2)}) collective-permute-start(bf16[136,256]{1,0:T(8,128)(2,1)S(1)} %get-tuple-element.11.refs_3_), channel_id=1, source_target_pairs={{0,4},{8,12},{16,20},{24,28},{32,36},{40,44},{48,52},{56,60},{64,6... | collective-permute-start | bytes 208904 | tf_op jit(solution)/shard_map/ppermute | solution.py:216
